TPU v7x, 32 devices: a whole 2x2x4 slice. The times are simulated.
32 devices in a mesh: seq: 2 (over core), hid: 4 (over y, x), wid: 4 (over z).
Axes of the slice: x: 2, y: 2, z: 4, core: 2. Of those that a mesh axis runs over, the one named last changes fastest.
Arguments:
- inputs: bfloat16 [2048, 1536], P(('seq', 'hid'), 'wid'), may hold values from -6 to 6
- gain_attn: bfloat16 [1536], P('wid'), may hold values from 0.5 to 1.5
- gain_ffn: bfloat16 [1536], P('wid'), may hold values from 0.5 to 1.5
- w_query: bfloat16 [1536, 1536], P(None, 'wid'), may hold values from -0.15625 to 0.15625
- w_key: bfloat16 [1536, 1536], P(None, 'wid'), may hold values from -0.15625 to 0.15625
- w_value: bfloat16 [1536, 1536], P(None, 'wid'), may hold values from -0.15625 to 0.15625
- w_house: bfloat16 [1536, 1536], P(None, 'wid'), may hold values from -0.15625 to 0.15625
- w_beta: bfloat16 [1536, 12], P(None, 'wid'), may hold values from -0.15625 to 0.15625
- w_out: bfloat16 [1536, 1536], P('wid'), may hold values from -0.625 to 0.625
- w_gate: bfloat16 [1536, 4096], P(None, ('hid', 'wid')), may hold values from -0.15625 to 0.15625
- w_up: bfloat16 [1536, 4096], P(None, ('hid', 'wid')), may hold values from -0.15625 to 0.15625
- w_down: bfloat16 [4096, 1536], P(('hid', 'wid')), may hold values from -0.09375 to 0.09375
- lengths: int32 [3], replicated, may hold values from 1 to 1024, 2048 in all
- cotangent: bfloat16 [2048, 1536], P(('seq', 'hid'), 'wid'), may hold values from -6 to 6
Outputs:
- output: bfloat16 [2048, 1536], P(('seq', 'hid'), 'wid')
- d_inputs: float32 [2048, 1536], P(('seq', 'hid'), 'wid')
- d_gain_attn: float32 [1536], P(('seq', 'hid'))
- d_gain_ffn: float32 [1536], P(('seq', 'hid'))
- d_query: float32 [1536, 1536], P(('seq', 'hid'), 'wid')
- d_key: float32 [1536, 1536], P(('seq', 'hid'), 'wid')
- d_value: float32 [1536, 1536], P(('seq', 'hid'), 'wid')
- d_house: float32 [1536, 1536], P(('seq', 'hid'), 'wid')
- d_beta: float32 [1536, 12], P(('seq', 'hid'), 'wid')
- d_out: float32 [1536, 1536], P('wid', ('seq', 'hid'))
- d_gate: float32 [1536, 4096], P('seq', ('hid', 'wid'))
- d_up: float32 [1536, 4096], P('seq', ('hid', 'wid'))
- d_down: float32 [4096, 1536], P(('hid', 'wid'), 'seq')
Inputs may be any that keep to these rules, and one draw needn't show every extreme that they name: `lengths`: the 3 documents are packed in order and fill all 2048 tokens; the longest has exactly 1024 tokens.
All inputs are finite; a program needn't handle non-finite values.
Results may differ from a plain program's by a relative error of at most 0.014.
Values may be sent and summed in bfloat16 or wider, within the bound.
A program may use at most 448 MiB of HBM per device.

v0:
```python
import functools
import types

import jax
import jax.numpy as jnp
from jax import lax
from jax.experimental import pallas as pl
from jax.experimental.pallas import tpu as pltpu
from jax.sharding import PartitionSpec as P

HDIM = 128
LEAST = 1024

eps_norm = 1e-06
neg_big = -1e30
BF = jnp.bfloat16
F32 = jnp.float32
VMEM_LIMIT = 60 * 1024 * 1024
VMEM_ALL = 67043328


def dot(a, b, ca, cb):
    return lax.dot_general(a, b, (((ca,), (cb,)), ((), ())), preferred_element_type=F32)


def split(a):
    hi = a.astype(BF)
    return hi, (a - hi.astype(F32)).astype(BF)


def dot3(a, b, ca, cb):
    return dot(a[0], b[0], ca, cb) + (dot(a[0], b[1], ca, cb) + dot(a[1], b[0], ca, cb))


def dot1(a, b, ca, cb):
    return dot(a.astype(BF), b.astype(BF), ca, cb)


def iotas(n):
    rows = lax.broadcasted_iota(jnp.int32, (n, n), 0)
    cols = lax.broadcasted_iota(jnp.int32, (n, n), 1)
    return rows, cols


def head_cols(h):
    return slice(h * HDIM, (h + 1) * HDIM)


def house_terms(raw, strength, heads, h):
    inv = lax.rsqrt(jnp.sum(raw * raw, -1, keepdims=True) + eps_norm)
    lane = lax.broadcasted_iota(jnp.int32, strength.shape, 1)
    c = jnp.sum(jnp.where(lane == h, strength, 0.0), 1, keepdims=True)
    root = jnp.sqrt(2.0 / (1.0 + jnp.exp(-c)))
    return inv, root


def path_fwd_stage(heads, q_ref, k_ref, r_ref, c_ref, qt_ref, kt_ref, near_ref, p_ref,
                   u_ref, inv_ref, psi_ref, x_ref, y_ref, done=None):
    n = c_ref.shape[0]
    rows, cols = iotas(n)
    strength = c_ref[...]
    us, us2, lows, invs = [], [], [], []
    for h in range(heads):
        raw = r_ref[:, head_cols(h)]
        inv, root = house_terms(raw, strength, heads, h)
        u = raw * (inv * root)
        u_ref[:, head_cols(h)] = u
        u2 = split(u)
        low = jnp.where(rows > cols, dot3(u2, u2, 1, 1), 0.0)
        us.append(u)
        us2.append(u2)
        lows.append(low)
        first = jnp.where(rows == cols, 1.0, 0.0) - jnp.where(rows // 2 == cols // 2, low, 0.0)
        invs.append(first)
    span = 2
    while span < n:
        pick = (rows // (2 * span) == cols // (2 * span)) & (rows // span != cols // span)
        halves = [split(m) for m in invs]
        mids = [dot3(split(jnp.where(pick, lows[h], 0.0)), halves[h], 1, 0) for h in range(heads)]
        invs = [invs[h] - dot3(halves[h], split(mids[h]), 1, 0) for h in range(heads)]
        span = span * 2
    for h in range(heads):
        inv_ref[h] = invs[h]
        kin = split(invs[h])
        q = q_ref[:, head_cols(h)]
        k = k_ref[:, head_cols(h)]
        q2, k2, u2 = split(q), split(k), us2[h]
        a = jnp.where(rows > cols, dot3(u2, k2, 1, 1), 0.0)
        aq = jnp.where(rows < cols, dot3(k2, u2, 1, 1), 0.0)
        fq = jnp.where(rows >= cols, dot3(q2, u2, 1, 1), 0.0)
        fq2 = split(fq)
        x = dot3(kin, u2, 1, 0)
        y = dot3(kin, u2, 0, 0)
        psi = dot3(kin, split(a), 1, 0)
        x2 = split(x)
        x_ref[:, head_cols(h)] = x
        y_ref[:, head_cols(h)] = y
        psi_ref[h] = psi
        qt_ref[:, head_cols(h)] = (q - dot3(fq2, x2, 1, 0)).astype(BF)
        kt_ref[:, head_cols(h)] = (k - dot3(split(aq), split(y), 1, 0)).astype(BF)
        near_ref[h] = dot3(q2, k2, 1, 1) - dot3(fq2, split(psi), 1, 0)
        er, ec = iotas(HDIM)
        p_ref[h] = (jnp.where(er == ec, 1.0, 0.0) - dot3(u2, x2, 0, 0)).astype(p_ref.dtype)
        if done is not None:
            done(h)


def path_fwd_kernel(heads, *refs):
    path_fwd_stage(heads, *refs)


def path_fwd(q, k, r, c, heads):
    n, width = q.shape
    flat = jax.ShapeDtypeStruct((n, width), F32)
    low = jax.ShapeDtypeStruct((n, width), BF)
    square = jax.ShapeDtypeStruct((heads, n, n), F32)
    return pl.pallas_call(
        functools.partial(path_fwd_kernel, heads),
        out_shape=(low, low, square, jax.ShapeDtypeStruct((heads, HDIM, HDIM), F32),
                   flat, square, square, flat, flat),
        compiler_params=pltpu.CompilerParams(vmem_limit_bytes=VMEM_LIMIT),
        name="path_fwd",
    )(q, k, r, c)


def doc_of(pos, len_ref):
    total = len_ref[0]
    doc = (pos >= total).astype(jnp.int32)
    for i in range(1, len_ref.shape[0]):
        total = total + len_ref[i]
        doc = doc + (pos >= total).astype(jnp.int32)
    return doc


def chain_slot(r, m):
    return r * (r - 1) // 2 + m


def attn_fwd_stage(heads, hops, row, len_ref, qt_ref, near_ref, v_ref, fv_ref, fp_ref, chain_ref,
                   o_ref, p_ref, s_ref, get_k, get_p):
    n = qt_ref.shape[0]
    scale = HDIM ** (-0.5)
    rows, cols = iotas(n)
    own = doc_of(row * n + rows, len_ref)
    near_ok = (rows >= cols) & (own == doc_of(row * n + cols, len_ref))
    for h in range(heads):
        cs = head_cols(h)
        q = qt_ref[:, cs]
        for copy in get_k[h] + get_p[h]:
            copy.wait_recv()
        s = jnp.where(near_ok, near_ref[h] * scale, neg_big)
        s_ref[0:n, :] = s
        top = jnp.max(s, 1, keepdims=True)
        for r in range(1, hops + 1):
            keys = chain_ref[chain_slot(r, 0), :, cs]
            for m in range(1, r):
                keys = dot(keys, fp_ref[r - m - 1, h].astype(BF), 1, 1).astype(BF)
                chain_ref[chain_slot(r, m), :, cs] = keys
            source = row - r
            docs = jnp.where(source >= 0, doc_of(source * n + cols, len_ref), -1)
            s = jnp.where(own == docs, dot(q, keys, 1, 1) * scale, neg_big)
            s_ref[r * n:(r + 1) * n, :] = s
            top = jnp.maximum(top, jnp.max(s, 1, keepdims=True))
        total = jnp.zeros((n, 1), F32)
        for r in range(hops + 1):
            e = jnp.exp(s_ref[r * n:(r + 1) * n, :] - top)
            s_ref[r * n:(r + 1) * n, :] = e
            total = total + jnp.sum(e, 1, keepdims=True)
        recip = 1.0 / total
        out = jnp.zeros((n, HDIM), F32)
        for r in range(hops + 1):
            p = (s_ref[r * n:(r + 1) * n, :] * recip).astype(BF)
            p_ref[r, h] = p
            vals = v_ref[:, cs] if r == 0 else fv_ref[r - 1, :, cs]
            out = out + dot(p, vals, 1, 0)
        o_ref[:, cs] = out.astype(BF)

def attn_fwd_kernel(heads, hops, len_ref, row_ref, qt_ref, near_ref, v_ref, fk_ref, fv_ref, fp_ref,
                    o_ref, p_ref, chain_ref, s_ref):
    for r in range(1, hops + 1):
        chain_ref[chain_slot(r, 0)] = fk_ref[r - 1]
    none = [[] for _ in range(heads)]
    attn_fwd_stage(heads, hops, row_ref[0], len_ref, qt_ref, near_ref, v_ref, fv_ref, fp_ref, chain_ref,
                   o_ref, p_ref, s_ref, none, none)


def attn_fwd(lengths, my_row, qt, near, v, far_k, far_v, far_p, heads, hops):
    n, width = qt.shape
    slots = hops * (hops + 1) // 2
    smem = pl.BlockSpec(memory_space=pltpu.SMEM)
    vmem = pl.BlockSpec(memory_space=pltpu.VMEM)
    return pl.pallas_call(
        functools.partial(attn_fwd_kernel, heads, hops),
        in_specs=[smem, smem] + [vmem] * 6,
        out_shape=(
            jax.ShapeDtypeStruct((n, width), BF),
            jax.ShapeDtypeStruct((hops + 1, heads, n, n), BF),
            jax.ShapeDtypeStruct((slots, n, width), BF),
        ),
        scratch_shapes=[pltpu.VMEM(((hops + 1) * n, n), F32)],
        compiler_params=pltpu.CompilerParams(vmem_limit_bytes=VMEM_LIMIT),
        name="attn_fwd",
    )(lengths, my_row, qt, near, v, far_k, far_v, far_p)


def attn_bwd_kernel(heads, hops, p_ref, go_ref, qt_ref, v_ref, fv_ref, fp_ref, chain_ref,
                    gqt_ref, gnear_ref, gv_ref, sendk_ref, sendv_ref, sendp_ref, dp_ref):
    n = qt_ref.shape[0]
    scale = HDIM ** (-0.5)
    for h in range(heads):
        cs = head_cols(h)
        go = go_ref[:, cs]
        q = qt_ref[:, cs]
        delta = jnp.zeros((n, 1), F32)
        for r in range(hops + 1):
            vals = v_ref[:, cs] if r == 0 else fv_ref[r - 1, :, cs]
            dp = dot(go, vals, 1, 1)
            dp_ref[r] = dp
            delta = delta + jnp.sum(p_ref[r, h].astype(F32) * dp, 1, keepdims=True)
            gv = dot(p_ref[r, h], go, 0, 0)
            if r == 0:
                gv_ref[:, cs] = gv
            else:
                sendv_ref[r - 1, :, cs] = gv.astype(BF)
        gnear_ref[h] = p_ref[0, h].astype(F32) * (dp_ref[0] - delta) * scale
        gq = jnp.zeros((n, HDIM), F32)
        gps = [jnp.zeros((HDIM, HDIM), F32) for _ in range(hops - 1)]
        for r in range(1, hops + 1):
            gs = (p_ref[r, h].astype(F32) * (dp_ref[r] - delta) * scale).astype(BF)
            gq = gq + dot(gs, chain_ref[chain_slot(r, r - 1), :, cs], 1, 0)
            gk = dot(gs, q, 0, 0)
            for m in range(r - 1, 0, -1):
                back = r - m - 1
                gkb = gk.astype(BF)
                gps[back] = gps[back] + dot(gkb, chain_ref[chain_slot(r, m - 1), :, cs], 0, 0)
                gk = dot(gkb, fp_ref[back, h].astype(BF), 1, 0)
            sendk_ref[r - 1, :, cs] = gk.astype(BF)
        gqt_ref[:, cs] = gq
        for i in range(hops - 1):
            sendp_ref[i, h] = gps[i].astype(BF)


def attn_bwd(p, go, qt, v, far_v, far_p, chain, heads, hops):
    n, width = qt.shape
    return pl.pallas_call(
        functools.partial(attn_bwd_kernel, heads, hops),
        out_shape=(
            jax.ShapeDtypeStruct((n, width), F32),
            jax.ShapeDtypeStruct((heads, n, n), F32),
            jax.ShapeDtypeStruct((n, width), F32),
            jax.ShapeDtypeStruct((hops, n, width), BF),
            jax.ShapeDtypeStruct((hops, n, width), BF),
            jax.ShapeDtypeStruct((hops - 1, heads, HDIM, HDIM), BF),
        ),
        scratch_shapes=[pltpu.VMEM((hops + 1, n, n), F32)],
        compiler_params=pltpu.CompilerParams(vmem_limit_bytes=VMEM_LIMIT),
        name="attn_bwd",
    )(p, go, qt, v, far_v, far_p, chain)


def path_bwd_kernel(heads, q_ref, k_ref, r_ref, c_ref, u_ref, inv_ref, psi_ref, x_ref, y_ref,
                    gqt_ref, gkt_ref, gnear_ref, gp_ref, gq_ref, gk_ref, gr_ref, gc_ref):
    n = q_ref.shape[0]
    rows, cols = iotas(n)
    strength = c_ref[...]
    lane = lax.broadcasted_iota(jnp.int32, strength.shape, 1)
    gc_all = jnp.zeros(strength.shape, F32)
    for h in range(heads):
        cs = head_cols(h)
        q, k, u = q_ref[:, cs], k_ref[:, cs], u_ref[:, cs]
        qb, kb, ub = q.astype(BF), k.astype(BF), u.astype(BF)
        kin = inv_ref[h].astype(BF)
        psi = psi_ref[h].astype(BF)
        x, y = x_ref[:, cs].astype(BF), y_ref[:, cs].astype(BF)
        gqt, gkt = gqt_ref[:, cs], gkt_ref[:, cs]
        gqtb, gktb = gqt.astype(BF), gkt.astype(BF)
        gs = gnear_ref[h]
        gsb = gs.astype(BF)
        gst = gs.T.astype(BF)
        gp = gp_ref[h].astype(BF)
        f = jnp.where(rows <= cols, dot(ub, qb, 1, 1), 0.0).astype(BF)
        fq = jnp.where(rows >= cols, dot(qb, ub, 1, 1), 0.0).astype(BF)
        a = jnp.where(rows > cols, dot(ub, kb, 1, 1), 0.0).astype(BF)
        gx = -(dot(f, gqtb, 1, 0) + dot(ub, gp, 1, 0))
        gy = -dot(a, gktb, 1, 0)
        phiq = dot(fq, kin, 1, 0).astype(BF)
        back = dot(gst, phiq, 1, 0)
        backb = back.astype(BF)
        gfq = jnp.where(rows >= cols, -(dot(gqtb, x, 1, 1) + dot(gsb, psi, 1, 1)), 0.0)
        gaq = jnp.where(rows < cols, -(dot(gktb, y, 1, 1) + back), 0.0)
        kgx = dot(kin, gx.astype(BF), 0, 0)
        kgy = dot(kin, gy.astype(BF), 1, 0)
        zt = dot(x, kgx.astype(BF), 1, 1) + dot(kgy.astype(BF), y, 1, 1) - dot(psi, backb, 1, 0)
        glt = jnp.where(rows < cols, -zt, 0.0)
        sym = (glt + glt.T).astype(BF)
        gfqb, gaqb = gfq.astype(BF), gaq.astype(BF)
        gu = (kgx + kgy - dot(x, gp, 1, 1) + dot(gfq.T.astype(BF), qb, 1, 0)
              + dot(gaq.T.astype(BF), kb, 1, 0) + dot(sym, ub, 1, 0))
        gq_ref[:, cs] = (gqt + dot(gsb, kb, 1, 0) + dot(gfqb, ub, 1, 0)).astype(BF)
        gk_ref[:, cs] = (gkt + dot(gst, qb, 1, 0) + dot(gaqb, ub, 1, 0)).astype(BF)
        raw = r_ref[:, cs]
        inv, root = house_terms(raw, strength, heads, h)
        gc = jnp.sum(gu * u, 1, keepdims=True) * (1.0 - 0.5 * root * root) * 0.5
        gun = gu * root
        un = raw * inv
        gr = inv * (gun - un * jnp.sum(gun * un, 1, keepdims=True))
        gr_ref[:, cs] = gr.astype(BF)
        gc_all = jnp.where(lane == h, gc, gc_all)
    gc_ref[...] = gc_all.astype(BF)


def path_bwd(q, k, r, c, saved, gqt, gkt, gnear, gp, heads):
    n, width = q.shape
    low = jax.ShapeDtypeStruct((n, width), BF)
    return pl.pallas_call(
        functools.partial(path_bwd_kernel, heads),
        out_shape=(low, low, low, jax.ShapeDtypeStruct((n, heads), BF)),
        compiler_params=pltpu.CompilerParams(vmem_limit_bytes=VMEM_LIMIT),
        name="path_bwd",
    )(q, k, r, c, *saved, gqt, gkt, gnear, gp)


MESH = pl.DeviceIdType.MESH


class Copies:
    def __init__(self, send, recv):
        self.send, self.recv, self.count, self.open = send, recv, 0, []

    def start(self, src, dst, device):
        i = self.count
        self.count = i + 1
        copy = pltpu.make_async_remote_copy(
            src_ref=src, dst_ref=dst, send_sem=self.send.at[i], recv_sem=self.recv.at[i],
            device_id=device, device_id_type=MESH)
        copy.start()
        self.open.append(copy)
        return copy

    def sent(self, some):
        for copy in some:
            copy.wait_send()
        self.open = [copy for copy in self.open if all(copy is not other for other in some)]


class Loads:
    def __init__(self, sems):
        self.sems, self.count = sems, 0

    def start(self, src, dst):
        copy = pltpu.make_async_copy(src, dst, self.sems.at[self.count])
        self.count = self.count + 1
        copy.start()
        return copy


class Place:
    def __init__(self, sizes):
        self.seq_n, self.hid_n, self.wid_n = sizes
        self.seq = lax.axis_index("seq")
        self.hid = lax.axis_index("hid")
        self.wid = lax.axis_index("wid")
        self.rows_n = self.seq_n * self.hid_n
        self.row = self.seq * self.hid_n + self.hid

    def wid_peer(self, i):
        return lax.rem(self.wid + i, self.wid_n)

    def hid_peer(self, i):
        return lax.rem(self.hid + i, self.hid_n)

    def seq_peer(self, i):
        return lax.rem(self.seq + i, self.seq_n)

    def row_peer(self, i):
        to = lax.rem(self.row + i + self.rows_n, self.rows_n)
        return {"seq": to // self.hid_n, "hid": lax.rem(to, self.hid_n)}

    def barrier(self):
        sem = pltpu.get_barrier_semaphore()
        for i in range(1, self.wid_n):
            pl.semaphore_signal(sem, inc=1, device_id={"wid": self.wid_peer(i)}, device_id_type=MESH)
        for i in range(1, self.rows_n):
            pl.semaphore_signal(sem, inc=1, device_id=self.row_peer(i), device_id_type=MESH)
        pl.semaphore_wait(sem, self.wid_n - 1 + self.rows_n - 1)


def aligned(start, size, step):
    return pl.ds(pl.multiple_of(start, step), size)


def attn_bwd_head(hops, h, p_ref, go, qt_ref, v_ref, fv_ref, fp_ref, chain_ref,
                  gqt_ref, gnear_ref, gv_ref, sendk_ref, sendv_ref, sendp_ref, dp_ref):
    n = qt_ref.shape[0]
    scale = HDIM ** (-0.5)
    cs = head_cols(h)
    q = qt_ref[:, cs]
    delta = jnp.zeros((n, 1), F32)
    for r in range(hops + 1):
        vals = v_ref[:, cs] if r == 0 else fv_ref[r - 1, :, cs]
        dp = dot(go, vals, 1, 1)
        dp_ref[r * n:(r + 1) * n, :] = dp
        delta = delta + jnp.sum(p_ref[r, h].astype(F32) * dp, 1, keepdims=True)
        gv = dot(p_ref[r, h], go, 0, 0)
        if r == 0:
            gv_ref[:, cs] = gv
        else:
            sendv_ref[r - 1, :, cs] = gv.astype(BF)
    gnear_ref[h] = p_ref[0, h].astype(F32) * (dp_ref[0:n, :] - delta) * scale
    gq = jnp.zeros((n, HDIM), F32)
    gps = [jnp.zeros((HDIM, HDIM), F32) for _ in range(hops - 1)]
    for r in range(1, hops + 1):
        gs = (p_ref[r, h].astype(F32) * (dp_ref[r * n:(r + 1) * n, :] - delta) * scale).astype(BF)
        gq = gq + dot(gs, chain_ref[chain_slot(r, r - 1), :, cs], 1, 0)
        gk = dot(gs, q, 0, 0)
        for m in range(r - 1, 0, -1):
            back = r - m - 1
            gkb = gk.astype(BF)
            gps[back] = gps[back] + dot(gkb, chain_ref[chain_slot(r, m - 1), :, cs], 0, 0)
            gk = dot(gkb, fp_ref[back, h].astype(BF), 1, 0)
        sendk_ref[r - 1, :, cs] = gk.astype(BF)
    gqt_ref[:, cs] = gq
    for i in range(hops - 1):
        sendp_ref[i, h] = gps[i].astype(BF)


def path_bwd_head(h, heads, q_ref, k_ref, r_ref, c_ref, u_ref, inv_ref, psi_ref, x_ref, y_ref,
                  gqt, gkt, gs, gp):
    n = c_ref.shape[0]
    rows, cols = iotas(n)
    cs = head_cols(h)
    q, k, u = q_ref[:, cs], k_ref[:, cs], u_ref[:, cs]
    qb, kb, ub = q.astype(BF), k.astype(BF), u.astype(BF)
    kin = inv_ref[h].astype(BF)
    psi = psi_ref[h].astype(BF)
    x, y = x_ref[:, cs].astype(BF), y_ref[:, cs].astype(BF)
    gqtb, gktb = gqt.astype(BF), gkt.astype(BF)
    gsb = gs.astype(BF)
    gst = gs.T.astype(BF)
    gp = gp.astype(BF)
    f = jnp.where(rows <= cols, dot(ub, qb, 1, 1), 0.0).astype(BF)
    fq = jnp.where(rows >= cols, dot(qb, ub, 1, 1), 0.0).astype(BF)
    a = jnp.where(rows > cols, dot(ub, kb, 1, 1), 0.0).astype(BF)
    gx = -(dot(f, gqtb, 1, 0) + dot(ub, gp, 1, 0))
    gy = -dot(a, gktb, 1, 0)
    phiq = dot(fq, kin, 1, 0).astype(BF)
    back = dot(gst, phiq, 1, 0)
    backb = back.astype(BF)
    gfq = jnp.where(rows >= cols, -(dot(gqtb, x, 1, 1) + dot(gsb, psi, 1, 1)), 0.0)
    gaq = jnp.where(rows < cols, -(dot(gktb, y, 1, 1) + back), 0.0)
    kgx = dot(kin, gx.astype(BF), 0, 0)
    kgy = dot(kin, gy.astype(BF), 1, 0)
    zt = dot(x, kgx.astype(BF), 1, 1) + dot(kgy.astype(BF), y, 1, 1) - dot(psi, backb, 1, 0)
    glt = jnp.where(rows < cols, -zt, 0.0)
    sym = (glt + glt.T).astype(BF)
    gfqb, gaqb = gfq.astype(BF), gaq.astype(BF)
    gu = (kgx + kgy - dot(x, gp, 1, 1) + dot(gfq.T.astype(BF), qb, 1, 0)
          + dot(gaq.T.astype(BF), kb, 1, 0) + dot(sym, ub, 1, 0))
    gq = (gqt + dot(gsb, kb, 1, 0) + dot(gfqb, ub, 1, 0)).astype(BF)
    gk = (gkt + dot(gst, qb, 1, 0) + dot(gaqb, ub, 1, 0)).astype(BF)
    raw = r_ref[:, cs]
    inv, root = house_terms(raw, c_ref[...], heads, h)
    gc = jnp.sum(gu * u, 1, keepdims=True) * (1.0 - 0.5 * root * root) * 0.5
    gun = gu * root
    un = raw * inv
    gr = (inv * (gun - un * jnp.sum(gun * un, 1, keepdims=True))).astype(BF)
    return gq, gk, gr, gc


class Heads:
    def __init__(self, ref, kind):
        self.ref, self.kind = ref, kind

    def __getitem__(self, index):
        base = 3 * index[1].start + self.kind * HDIM
        return self.ref[index[0], base:base + HDIM]


def turned(index, by):
    low = index % 2
    high = index // 2 % 2
    return index + (1 - 2 * low) * (by % 2) + (2 - 4 * high) * (by // 2)


def step_kernel(cfg, names, *refs):
    heads, hops, sizes = cfg
    R = types.SimpleNamespace(**dict(zip(names, refs)))
    place = Place(sizes)
    wid_n, hid_n, seq_n = place.wid_n, place.hid_n, place.seq_n
    n, col = R.x.shape
    width = heads * HDIM
    model = R.act.shape[1]
    ff = R.wg.shape[1]
    sub = n // wid_n
    half = model // seq_n
    piece = model // place.rows_n
    copies, loads = Copies(R.send_sem, R.recv_sem), Loads(R.load_sem)
    my_cols = aligned(place.wid * col, col, 128)
    my_rows = aligned(place.wid * sub, sub, sub)
    mine = aligned(place.seq * half, half, 128)
    other = aligned((1 - place.seq) * half, half, 128)
    sibling = {"seq": 1 - place.seq}
    order = sorted(range(1, wid_n), key=lambda i: -min(i, wid_n - i))
    to_wid = [{"wid": place.wid_peer(i)} for i in order]
    near = [{"hid": turned(place.hid, j)} for j in range(hid_n)]

    load_x = [loads.start(R.x, R.xall.at[:, my_cols])]
    load_v = loads.start(R.wv, R.w_s.at[:, pl.ds(3 * width, width)])
    load_w = [loads.start(w.at[:, pl.ds(h * HDIM, HDIM)], R.w_s.at[:, pl.ds((3 * h + m) * HDIM, HDIM)])
              for h in range(heads) for m, w in enumerate((R.wq, R.wk, R.wr))]
    load_dy = loads.start(R.dy, R.dyall.at[:, my_cols])
    load_o = loads.start(R.wo, R.wo_s)
    load_f = [loads.start(R.wg, R.wg_s.at[:, pl.ds(0, ff)]), loads.start(R.wu, R.wu_s.at[:, pl.ds(0, ff)]),
              loads.start(R.wd, R.wd_s.at[pl.ds(0, ff), :])]
    R.gain_in[0:1, :] = R.gain_attn[...].astype(F32).reshape(1, col)
    R.gain_in[1:2, :] = R.gain_ffn[...].astype(F32).reshape(1, col)
    place.barrier()

    get_x = [copies.start(R.x, R.xall.at[:, my_cols], d) for d in to_wid]
    get_x += [copies.start(R.gain_in, R.gall.at[:, my_cols], d) for d in to_wid]
    R.gall[:, my_cols] = R.gain_in[...]

    part_f = ff // seq_n
    mine_c = aligned(place.seq * half, half, 16)
    mine_f = aligned(place.seq * part_f, part_f, 16)

    def cols_of(j):
        return pl.ds(j * ff, ff)

    def down_rows(j, piece_i=0, pieces=1):
        size = part_f // pieces
        return aligned(j * ff + place.seq * part_f + piece_i * size, size, 16)

    def pass_on(ref, device):
        return copies.start(ref, ref, device)

    get_gate = [copies.start(R.wg.at[mine_c, :], R.wg_s.at[mine_c, cols_of(j)], near[j]) for j in (1, 2)]
    for copy in get_gate:
        copy.wait_recv()
    get_gate3 = copies.start(R.wg_s.at[mine_c, cols_of(1)], R.wg_s.at[mine_c, cols_of(3)], near[2])

    for copy in load_x:
        copy.wait()
    for copy in get_x:
        copy.wait_recv()
    get_dy = [copies.start(R.dy, R.dyall.at[:, my_cols], d) for d in to_wid]
    xf = R.xall[...].astype(F32)
    inv_rms = lax.rsqrt(jnp.mean(xf * xf, -1, keepdims=True) + eps_norm)
    R.inv_rms[...] = inv_rms
    R.act[...] = (xf * inv_rms * R.gall[0:1, :]).astype(BF)
    load_v.wait()
    R.v[...] = dot(R.act[...], R.w_s[:, 3 * width:4 * width], 1, 0).astype(BF)
    get_v = [copies.start(R.v, R.fv.at[i - 1], place.row_peer(i)) for i in range(1, hops + 1)]
    for copy in load_w:
        copy.wait()
    R.proj[...] = dot(R.act[...], R.w_s[:, 0:3 * width], 1, 0)
    R.c[...] = dot(R.act[...], R.wb[...], 1, 1)

    get_k = [[] for _ in range(heads)]
    get_p = [[] for _ in range(heads)]

    def send_head(h):
        cs = head_cols(h)
        for i in range(1, hops + 1):
            get_k[h].append(copies.start(R.kt_s.at[:, cs], R.chain.at[chain_slot(i, 0), :, cs], place.row_peer(i)))
        for i in range(1, hops):
            get_p[h].append(copies.start(R.prod_s.at[h], R.fp.at[i - 1, h], place.row_peer(i)))

    path_fwd_stage(heads, Heads(R.proj, 0), Heads(R.proj, 1), Heads(R.proj, 2), R.c, R.qt, R.kt_s, R.near_s, R.prod_s,
                   R.u, R.inv, R.psi, R.x1, R.y1, send_head)

    get_up = [copies.start(R.wu.at[mine_c, :], R.wu_s.at[mine_c, cols_of(j)], near[j]) for j in (1, 2)]
    get_down = [copies.start(R.wd.at[mine_f, :], R.wd_s.at[down_rows(j), :], near[j]) for j in (1, 2)]

    for copy in get_v:
        copy.wait_recv()
    attn_fwd_stage(heads, hops, place.row, R.lengths, R.qt, R.near_s, R.v, R.fv, R.fp, R.chain,
                   R.o, R.probs, R.s_s, get_k, get_p)

    load_o.wait()
    get_a = []
    for slot, i in enumerate(order):
        peer = place.wid_peer(i)
        rows = aligned(peer * sub, sub, sub)
        R.part_s[rows, :] = dot(R.o[rows, :], R.wo_s[...], 1, 0).astype(BF)
        get_a.append(copies.start(R.part_s.at[rows, :], R.recv_s.at[slot], {"wid": peer}))
    R.part_s[my_rows, :] = dot(R.o[my_rows, :], R.wo_s[...], 1, 0).astype(BF)
    for copy in get_up + get_down:
        copy.wait_recv()
    relay = [copies.start(R.wu_s.at[mine_c, cols_of(2)], R.wu_s.at[mine_c, cols_of(3)], near[1]),
             copies.start(R.wd_s.at[down_rows(1, 0, 2), :], R.wd_s.at[down_rows(3, 0, 2), :], near[2]),
             copies.start(R.wd_s.at[down_rows(2, 1, 2), :], R.wd_s.at[down_rows(3, 1, 2), :], near[1])]
    get_gate3.wait_recv()
    three = pl.ds(ff, 3 * ff)
    shared = [pass_on(R.wg_s.at[mine_c, three], sibling)]
    mixed = R.xall[my_rows, :].astype(F32) + R.part_s[my_rows, :].astype(F32)
    for slot, copy in enumerate(get_a):
        copy.wait_recv()
        mixed = mixed + R.recv_s[slot].astype(F32)
    R.mixed[...] = mixed
    inv_two = lax.rsqrt(jnp.mean(mixed * mixed, -1, keepdims=True) + eps_norm)
    R.row_s[...] = (mixed * inv_two * R.gall[1:2, :]).astype(BF)
    get_i = [copies.start(R.row_s, R.inner.at[my_rows, :], d) for d in to_wid]
    R.inner[my_rows, :] = R.row_s[...]
    for copy in relay:
        copy.wait_recv()
    shared.append(pass_on(R.wu_s.at[mine_c, three], sibling))
    shared += [pass_on(R.wd_s.at[down_rows(j), :], sibling) for j in (1, 2, 3)]
    twin_a = [copies.start(R.act.at[:, other], R.twin_act, sibling),
              copies.start(R.o, R.twin_o, sibling)]
    load_dy.wait()
    for copy in load_f:
        copy.wait()
    for copy in get_dy + shared + get_i:
        copy.wait_recv()

    def hidden_tile(t, carry):
        cs = aligned(t * ff, ff, 128)
        gate = dot(R.inner[...], R.wg_s[:, cs], 1, 0)
        up = dot(R.inner[...], R.wu_s[:, cs], 1, 0)
        g_hidden = dot(R.dyall[...], R.wd_s[cs, :], 1, 1)
        sig = 1.0 / (1.0 + jnp.exp(-gate))
        silu = gate * sig
        R.hidden[0:n, cs] = (silu * up).astype(BF)
        R.ggate[0:n, cs] = (g_hidden * up * sig * (1.0 + gate * (1.0 - sig))).astype(BF)
        R.gup[0:n, cs] = (g_hidden * silu).astype(BF)
        return carry

    lax.fori_loop(0, hid_n, hidden_tile, 0)

    twin = [copies.start(ref.at[pl.ds(0, n), :], ref.at[pl.ds(n, n), :], sibling)
            for ref in (R.hidden, R.ggate, R.gup)]
    twin += [copies.start(R.inner.at[:, other], R.twin_inner, sibling),
             copies.start(R.dyall.at[:, other], R.twin_dy, sibling)]

    def grad_tile(t, carry):
        cs = aligned(t * col, col, 128)
        R.gin[:, cs] = (dot(R.ggate[0:n, :], R.wg_s[cs, :], 1, 1)
                        + dot(R.gup[0:n, :], R.wu_s[cs, :], 1, 1)).astype(BF)
        return carry

    lax.fori_loop(0, wid_n, grad_tile, 0)
    get_g = []
    for slot, i in enumerate(order):
        peer = place.wid_peer(i)
        rows = aligned(peer * sub, sub, sub)
        get_g.append(copies.start(R.gin.at[rows, :], R.recv_s.at[slot], {"wid": peer}))

    copies.sent(shared + relay + [get_gate3] + get_a)
    for copy in twin:
        copy.wait_recv()
    R.left_t[:, 0:n] = R.inner[:, mine].T
    R.left_t[:, n:2 * n] = R.twin_inner[...].T
    down_a, down_b = pl.ds(0, half // 2), pl.ds(half // 2, half // 2)

    def grads_tile(j, carry):
        cs = aligned(j * ff, ff, 128)
        R.wg_s[0:half, cs] = dot(R.left_t[...], R.ggate[:, cs], 1, 0).astype(BF)
        R.wg_s[half:2 * half, cs] = dot(R.left_t[...], R.gup[:, cs], 1, 0).astype(BF)
        down = dot(R.hidden[0:n, cs], R.dyall[:, mine], 0, 0) + dot(R.hidden[n:2 * n, cs], R.twin_dy[...], 0, 0)
        R.wu_s[aligned(j * ff, ff, ff), 0:half] = down.astype(BF)
        return carry

    lax.fori_loop(0, hid_n, grads_tile, 0)
    upper, lower = pl.ds(0, half), pl.ds(half, half)

    def first_round(j, slot, rows, lanes, to, gus, downs):
        return [copies.start(R.wg_s.at[rows, cols_of(j)], gus.at[slot], to),
                copies.start(R.wu_s.at[cols_of(j), lanes], downs.at[slot], to)]

    get_r1 = (first_round(3, 1, upper, down_a, near[1], R.gu_x, R.dn_x)
              + first_round(3, 1, lower, down_b, near[2], R.gu_y, R.dn_y)
              + first_round(1, 0, upper, down_a, near[1], R.gu_x, R.dn_x)
              + first_round(2, 0, lower, down_b, near[2], R.gu_y, R.dn_y))

    def out_tile(t, carry):
        cs = aligned(t * col, col, 128)
        R.part_s[:, cs] = (dot(R.hidden[0:n, :], R.wd_s[:, cs], 1, 0) + R.part_s[:, cs].astype(F32)).astype(BF)
        return carry

    lax.fori_loop(0, wid_n, out_tile, 0)

    g_inner = R.gin[my_rows, :].astype(F32)
    for slot, copy in enumerate(get_g):
        copy.wait_recv()
        g_inner = g_inner + R.recv_s[slot].astype(F32)
    mixed = R.mixed[...]
    inv_two = lax.rsqrt(jnp.mean(mixed * mixed, -1, keepdims=True) + eps_norm)
    n_two = mixed * inv_two
    scaled = g_inner * R.gall[1:2, :]
    g_mixed = (R.dyall[my_rows, :].astype(F32)
               + inv_two * (scaled - n_two * jnp.mean(scaled * n_two, -1, keepdims=True)))
    R.row_g[...] = g_mixed.astype(BF)
    get_z = [copies.start(R.row_g, R.gz.at[my_rows, :], d) for d in to_wid]
    R.gz[my_rows, :] = R.row_g[...]
    R.gpart[1:2, :] = jnp.sum(g_inner * n_two, 0, keepdims=True)
    get_f = []
    for slot, i in enumerate(order):
        peer = place.wid_peer(i)
        get_f.append(copies.start(R.part_s.at[:, aligned(peer * col, col, 128)], R.recv_f.at[slot], {"wid": peer}))

    for copy in get_r1:
        copy.wait_recv()
    add_g = R.wg_s.at[upper, cols_of(2)]
    add_g[...] = (add_g[...].astype(F32) + R.gu_x[1].astype(F32)).astype(BF)
    add_u = R.wg_s.at[lower, cols_of(1)]
    add_u[...] = (add_u[...].astype(F32) + R.gu_y[1].astype(F32)).astype(BF)
    add_a = R.wu_s.at[cols_of(2), down_a]
    add_a[...] = (add_a[...].astype(F32) + R.dn_x[1].astype(F32)).astype(BF)
    add_b = R.wu_s.at[cols_of(1), down_b]
    add_b[...] = (add_b[...].astype(F32) + R.dn_y[1].astype(F32)).astype(BF)
    get_r2 = [copies.start(add_g, R.gu_x.at[2], near[2]), copies.start(add_a, R.dn_x.at[2], near[2]),
              copies.start(add_u, R.gu_y.at[2], near[1]), copies.start(add_b, R.dn_y.at[2], near[1])]

    for copy in twin_a:
        copy.wait_recv()
    for copy in get_z:
        copy.wait_recv()
    twin_z = copies.start(R.gz.at[:, other], R.twin_gz, sibling)

    gets = [[] for _ in range(heads)]
    for h in range(heads):
        cs = head_cols(h)
        go = dot(R.gz[...], R.wo_s[cs, :], 1, 1).astype(BF)
        attn_bwd_head(hops, h, R.probs, go, R.qt, R.v, R.fv, R.fp, R.chain,
                      R.gqt, R.near_s, R.gv, R.sendk, R.sendv, R.sendp, R.s_s)
        for i in range(1, hops + 1):
            to = place.row_peer(-i)
            gets[h].append(copies.start(R.sendv.at[i - 1, :, cs], R.recvv.at[i - 1, :, cs], to))
            gets[h].append(copies.start(R.sendk.at[i - 1, :, cs], R.recvk.at[i - 1, :, cs], to))
        for i in range(1, hops):
            gets[h].append(copies.start(R.sendp.at[i - 1, h], R.recvp.at[i - 1, h], place.row_peer(-i)))

    def left_of(ref, twin_ref):
        R.left_t[:, 0:n] = ref[:, mine].T
        R.left_t[:, n:2 * n] = twin_ref[...].T

    twin_z.wait_recv()
    left_of(R.gz, R.twin_gz)

    get_h = []

    def spread(src, dst):
        for j in range(1, hid_n):
            p = turned(place.hid, j)
            get_h.append(copies.start(src.at[aligned(p * piece, piece, 64), :], dst.at[j - 1], near[j]))

    R.wide_s[...] = dot(R.left_t[:, 0:n], R.o[...], 1, 0) + dot(R.left_t[:, n:2 * n], R.twin_o[...], 1, 0)
    R.d_out[...] = R.wide_s[aligned(place.hid * piece, piece, 64), :]
    R.send_o[...] = R.wide_s[...].astype(BF)
    spread(R.send_o, R.recv_o)
    left_of(R.act, R.twin_act)

    row8 = lax.broadcasted_iota(jnp.int32, (n, HDIM), 1)
    gc_all = jnp.zeros((n, HDIM), F32)
    for h in range(heads):
        for copy in gets[h]:
            copy.wait_recv()
        cs = head_cols(h)
        gv = R.gv[:, cs]
        for i in range(hops):
            gv = gv + R.recvv[i, :, cs].astype(F32)
        R.grads[0:n, (9 + h) * HDIM:(10 + h) * HDIM] = gv.astype(BF)
    val_cols = pl.ds(3 * width, width)
    twin_v = copies.start(R.grads.at[pl.ds(0, n), val_cols], R.grads.at[pl.ds(n, n), val_cols], sibling)
    twin_h = []

    def weights_of(slot, outs_of):
        cs = slice(slot * width, (slot + 1) * width)
        R.wide_s[...] = dot(R.left_t[...], R.grads[:, cs], 1, 0)
        R.wd_s[0:half, cs] = R.wide_s[...].astype(BF)
        own = R.wide_s[aligned(place.hid * piece, piece, 64), :]
        for m, (ref, at) in enumerate(outs_of):
            ref[:, at] = own[:, head_cols(m)]
        spread(R.wd_s.at[:, pl.ds(slot * width, width)], R.recv_q.at[:, :, pl.ds(slot * width, width)])

    def outs_of(h):
        return [(ref, head_cols(h)) for ref in (R.d_query, R.d_key, R.d_house)]

    val_outs = [(R.d_value, head_cols(m)) for m in range(heads)]
    for h in range(heads):
        cs = head_cols(h)
        gkt = R.recvk[0, :, cs].astype(F32)
        for i in range(1, hops):
            gkt = gkt + R.recvk[i, :, cs].astype(F32)
        gp = R.recvp[0, h].astype(F32)
        for i in range(1, hops - 1):
            gp = gp + R.recvp[i, h].astype(F32)
        gq, gk, gr, gc = path_bwd_head(h, heads, Heads(R.proj, 0), Heads(R.proj, 1), Heads(R.proj, 2), R.c,
                                       R.u, R.inv, R.psi, R.x1, R.y1, R.gqt[:, cs], gkt, R.near_s[h], gp)
        gc_all = jnp.where(row8 == h, gc, gc_all)
        for m, val in enumerate((gq, gk, gr)):
            R.grads[0:n, (3 * h + m) * HDIM:(3 * h + m + 1) * HDIM] = val
        gs = pl.ds(h * width, width)
        twin_h.append(copies.start(R.grads.at[pl.ds(0, n), gs], R.grads.at[pl.ds(n, n), gs], sibling))
        if h == 0:
            twin_v.wait_recv()
            weights_of(heads, val_outs)
        else:
            twin_h[h - 1].wait_recv()
            weights_of(h - 1, outs_of(h - 1))
    R.gcs[0:n, :] = gc_all.astype(BF)
    twin_c = copies.start(R.gcs.at[pl.ds(0, n), :], R.gcs.at[pl.ds(n, n), :], sibling)

    inv_rms = R.inv_rms[...]
    stat = jnp.zeros((n, 1), F32)
    get_n = []
    for slot, i in enumerate(order + [0]):
        peer = place.wid_peer(i)
        cs = aligned(peer * col, col, 128)
        g_act = dot(R.grads[0:n, :], R.w_s[cs, :], 1, 1) + dot(R.gcs[0:n, 0:heads], R.wb[:, cs], 1, 0)
        normed = R.xall[:, cs].astype(F32) * inv_rms
        both = g_act * normed
        stat = stat + jnp.sum(both * R.gall[0:1, cs], 1, keepdims=True)
        R.gpart[0:1, cs] = jnp.sum(both, 0, keepdims=True)
        if i == 0:
            R.own_n[...] = g_act
        else:
            R.send_n[slot] = g_act.astype(BF)
            get_n.append(copies.start(R.send_n.at[slot], R.recv_n.at[slot], {"wid": peer}))
    R.stat_s[...] = jnp.broadcast_to(stat, (n, HDIM)).T[0:8, :]
    get_s = [copies.start(R.stat_s, R.recv_st.at[slot], d) for slot, d in enumerate(to_wid)]
    twin_h[heads - 1].wait_recv()
    weights_of(heads - 1, outs_of(heads - 1))
    twin_c.wait_recv()
    d_beta = dot(R.gcs[0:n, :], R.act[:, mine], 0, 0) + dot(R.gcs[n:2 * n, :], R.twin_act[...], 0, 0)
    R.beta_s[...] = d_beta[0:8, :]

    def window(p):
        return aligned(p * piece // 128 * 128, 256, 128)

    get_b = [copies.start(R.beta_s.at[:, window(turned(place.hid, j))], R.recv_b.at[j - 1], near[j])
             for j in range(1, hid_n)]
    get_gain = [copies.start(R.gpart.at[:, window(lax.rem(place.row + i, place.rows_n))], R.recv_gain.at[i - 1],
                             place.row_peer(i)) for i in range(1, place.rows_n)]

    gain = R.gpart[:, window(place.row)]
    for i, copy in enumerate(get_gain):
        copy.wait_recv()
        gain = gain + R.recv_gain[i]
    R.gain_s[...] = gain
    get_gain2 = [copies.start(R.gain_s, R.recv_gain2.at[slot], d) for slot, d in enumerate(to_wid)]
    for copy in get_r2:
        copy.wait_recv()
    R.d_gate[...] = (R.wg_s[upper, 0:ff].astype(F32) + R.gu_x[0].astype(F32) + R.gu_x[2].astype(F32))
    R.d_up[...] = (R.wg_s[lower, 0:ff].astype(F32) + R.gu_y[0].astype(F32) + R.gu_y[2].astype(F32))
    for lanes, ref in ((down_a, R.dn_x), (down_b, R.dn_y)):
        R.d_down[:, lanes] = R.wu_s[0:ff, lanes].astype(F32) + ref[0].astype(F32) + ref[2].astype(F32)
    out = R.x[...].astype(F32) + R.part_s[:, my_cols].astype(F32)
    for slot, copy in enumerate(get_f):
        copy.wait_recv()
        out = out + R.recv_f[slot].astype(F32)
    R.output[...] = out.astype(BF)
    g_act = R.own_n[...]
    stats = R.stat_s[...]
    for slot in range(wid_n - 1):
        get_s[slot].wait_recv()
        get_n[slot].wait_recv()
        g_act = g_act + R.recv_n[slot].astype(F32)
        stats = stats + R.recv_st[slot]
    mean = stats.T[:, 0:1] / model
    normed = R.xall[:, my_cols].astype(F32) * inv_rms
    R.d_inputs[...] = (R.gz[:, my_cols].astype(F32)
                       + inv_rms * (g_act * R.gall[0:1, my_cols] - normed * mean))
    for copy in get_h + get_b:
        copy.wait_recv()
    for i in range(hid_n - 1):
        R.d_out[...] += R.recv_o[i].astype(F32)
    for slot, refs_of in [(heads, val_outs)] + [(h, outs_of(h)) for h in range(heads)]:
        for m, (ref, at) in enumerate(refs_of):
            base = slot * width + m * HDIM
            total = ref[:, at]
            for i in range(hid_n - 1):
                total = total + R.recv_q[i, :, base:base + HDIM].astype(F32)
            ref[:, at] = total
    d_beta = R.beta_s[:, window(place.hid)]
    for i in range(hid_n - 1):
        d_beta = d_beta + R.recv_b[i]
    gain = R.gain_s[...]
    for slot, copy in enumerate(get_gain2):
        copy.wait_recv()
        gain = gain + R.recv_gain2[slot]

    def exact(rows, at):
        return jnp.where(at % 2 == 1, rows[:, 64:64 + piece], rows[:, 0:piece])

    R.d_beta[...] = exact(d_beta, place.hid)[0:heads, :]
    R.gain_out[...] = exact(gain, place.row)
    copies.sent(copies.open)


def step(args, heads, hops, sizes):
    ins = ("lengths", "x", "dy", "gain_attn", "gain_ffn", "wq", "wk", "wv", "wr", "wb", "wo", "wg", "wu", "wd")
    shapes = dict(zip(ins, (a.shape for a in args)))
    n, col = shapes["x"]
    seq_n, hid_n, wid_n = sizes
    model, width = shapes["wq"]
    ff = shapes["wg"][1]
    sub = n // wid_n
    rows_n = seq_n * hid_n
    half = model // seq_n
    piece = model // rows_n
    slots = hops * (hops + 1) // 2
    S = jax.ShapeDtypeStruct
    V = pltpu.VMEM
    outs = dict(
        output=S((n, col), BF), d_inputs=S((n, col), F32), gain_out=S((8, piece), F32),
        d_query=S((piece, width), F32), d_key=S((piece, width), F32), d_value=S((piece, width), F32),
        d_house=S((piece, width), F32), d_beta=S((heads, piece), F32), d_out=S((piece, width), F32),
        d_gate=S((half, ff), F32), d_up=S((half, ff), F32), d_down=S((ff, half), F32),
    )
    peers_w, peers_h = wid_n - 1, hid_n - 1
    scratch = dict(
        gain_in=V((8, col), F32), gall=V((8, model), F32), inv_rms=V((n, 1), F32),
        act=V((n, model), BF), xall=V((n, model), BF), dyall=V((n, model), BF),
        proj=V((n, 3 * width), F32), c=V((n, heads), F32), v=V((n, width), BF),
        qt=V((n, width), BF), u=V((n, width), F32), inv=V((heads, n, n), F32), psi=V((heads, n, n), F32),
        x1=V((n, width), F32), y1=V((n, width), F32),
        fv=V((hops, n, width), BF), fp=V((hops - 1, heads, HDIM, HDIM), BF), chain=V((slots, n, width), BF),
        probs=V((hops + 1, heads, n, n), BF), o=V((n, width), BF), mixed=V((sub, model), F32),
        inner=V((n, model), BF), hidden=V((2 * n, hid_n * ff), BF), ggate=V((2 * n, hid_n * ff), BF),
        gup=V((2 * n, hid_n * ff), BF), gin=V((n, model), BF),
        w_s=V((model, 4 * width), BF), wo_s=V((width, model), BF),
        wg_s=V((model, hid_n * ff), BF), wu_s=V((model, hid_n * ff), BF), wd_s=V((hid_n * ff, model), BF),
        kt_s=V((n, width), BF), near_s=V((heads, n, n), F32), prod_s=V((heads, HDIM, HDIM), BF),
        s_s=V(((hops + 1) * n, n), F32), part_s=V((n, model), BF), recv_s=V((peers_w, sub, model), BF),
        row_s=V((sub, model), BF), row_g=V((sub, model), BF),
        twin_inner=V((n, half), BF), twin_dy=V((n, half), BF), twin_act=V((n, half), BF), twin_o=V((n, width), BF),
        twin_gz=V((n, half), BF), left_t=V((half, 2 * n), BF),
        gu_x=V((3, half, ff), BF), gu_y=V((3, half, ff), BF),
        dn_x=V((3, ff, half // 2), BF), dn_y=V((3, ff, half // 2), BF),
        gz=V((n, model), BF), gpart=V((8, model), F32), recv_f=V((peers_w, n, col), BF),
        gqt=V((n, width), F32), gv=V((n, width), F32),
        sendk=V((hops, n, width), BF), sendv=V((hops, n, width), BF), sendp=V((hops - 1, heads, HDIM, HDIM), BF),
        recvk=V((hops, n, width), BF), recvv=V((hops, n, width), BF), recvp=V((hops - 1, heads, HDIM, HDIM), BF),
        send_o=V((half, width), BF), recv_o=V((peers_h, piece, width), BF),
        grads=V((2 * n, 4 * width), BF), gcs=V((2 * n, HDIM), BF), wide_s=V((half, width), F32),
        recv_q=V((peers_h, piece, 4 * width), BF), beta_s=V((8, half), F32), recv_b=V((peers_h, 8, 256), F32),
        own_n=V((n, col), F32), send_n=V((peers_w, n, col), BF), recv_n=V((peers_w, n, col), BF),
        stat_s=V((8, n), F32), recv_st=V((peers_w, 8, n), F32),
        recv_gain=V((rows_n - 1, 8, 256), F32), gain_s=V((8, 256), F32), recv_gain2=V((peers_w, 8, 256), F32),
    )
    n_copies = 200
    scratch.update(load_sem=pltpu.SemaphoreType.DMA((24,)), send_sem=pltpu.SemaphoreType.DMA((n_copies,)),
                   recv_sem=pltpu.SemaphoreType.DMA((n_copies,)))
    spaces = {"lengths": pltpu.SMEM, "x": pltpu.VMEM, "gain_attn": pltpu.VMEM, "gain_ffn": pltpu.VMEM, "wb": pltpu.VMEM}
    vmem = pl.BlockSpec(memory_space=pltpu.VMEM)
    res = pl.pallas_call(
        functools.partial(step_kernel, (heads, hops, sizes), ins + tuple(outs) + tuple(scratch)),
        in_specs=[pl.BlockSpec(memory_space=spaces.get(i, pl.ANY)) for i in ins],
        out_shape=tuple(outs.values()),
        out_specs=tuple(vmem for _ in outs),
        scratch_shapes=list(scratch.values()),
        compiler_params=pltpu.CompilerParams(
            vmem_limit_bytes=VMEM_ALL, collective_id=1, has_side_effects=True),
        name="step",
    )(*args)
    return dict(zip(outs, res))


def finish_kernel(count, *refs):
    ins, outs, bufs, sems = refs[:count], refs[count:2 * count], refs[2 * count:3 * count], refs[3 * count]
    loads = [pltpu.make_async_copy(a, b, sems.at[0, i]) for i, (a, b) in enumerate(zip(ins, bufs))]
    stores = [pltpu.make_async_copy(b, c, sems.at[1, i]) for i, (b, c) in enumerate(zip(bufs, outs))]
    for copy in loads:
        copy.start()
    for load, store in zip(loads, stores):
        load.wait()
        store.start()
    for copy in stores:
        copy.wait()


def finish(arrays):
    count = len(arrays)
    spec = pl.BlockSpec(memory_space=pl.ANY)
    return pl.pallas_call(
        functools.partial(finish_kernel, count),
        in_specs=[spec] * count, out_specs=[spec] * count,
        out_shape=[jax.ShapeDtypeStruct(a.shape, a.dtype) for a in arrays],
        scratch_shapes=[pltpu.VMEM(a.shape, a.dtype) for a in arrays] + [pltpu.SemaphoreType.DMA((2, count))],
        compiler_params=pltpu.CompilerParams(vmem_limit_bytes=VMEM_ALL),
        name="finish",
    )(*arrays)


def shifted(array, axis, by):
    peers = lax.axis_size(axis)
    pairs = [(i, i + by) for i in range(peers) if 0 <= i + by < peers]
    return lax.ppermute(array, axis, pairs)


def norm_rows(hidden_f):
    inverse = lax.rsqrt(jnp.mean(hidden_f * hidden_f, -1, keepdims=True) + eps_norm)
    return (hidden_f * inverse, inverse)


def norm_back(grad_out, normed, inverse, gain_vec):
    scaled_grad = grad_out * gain_vec
    grad_gain = jnp.sum(grad_out * normed, 0)
    grad_in = inverse * (scaled_grad - normed * jnp.mean(scaled_grad * normed, -1, keepdims=True))
    return (grad_in, grad_gain)


ROWS = ("seq", "hid")


def body(inputs, gain_attn, gain_ffn, w_query, w_key, w_value, w_house, w_beta, w_out,
         w_gate, w_up, w_down, lengths, cotangent):
    tok, col = inputs.shape
    row_devs = lax.axis_size(ROWS)
    my_row = lax.axis_index(ROWS)
    my_wid = lax.axis_index("wid")
    wid_n = lax.axis_size("wid")
    tokens_all = tok * row_devs
    most_len = max(LEAST, 2 * tokens_all // 5)
    hops = min((most_len - 2) // tok + 1, row_devs - 1)
    heads = w_query.shape[1] // HDIM
    ff = w_gate.shape[1]
    sub = tok // wid_n

    x_all = lax.all_gather(inputs, "wid", axis=1, tiled=True)
    gain_one = lax.all_gather(gain_attn, "wid", axis=0, tiled=True).astype(F32)
    gain_two = lax.all_gather(gain_ffn, "wid", axis=0, tiled=True).astype(F32)
    dy_all = lax.all_gather(cotangent, "wid", axis=1, tiled=True)
    w_gu = lax.all_gather(jnp.concatenate([w_gate, w_up], 1), "hid", axis=0)
    w_dn = lax.all_gather(w_down, "hid", axis=0)
    model = x_all.shape[1]

    residual = x_all.astype(F32)
    normed_one, inverse_one = norm_rows(residual)
    act = (normed_one * gain_one).astype(BF)

    def project(weight):
        return jnp.dot(act, weight, preferred_element_type=F32)

    q, k, r, c = project(w_query), project(w_key), project(w_house), project(w_beta)
    v = project(w_value).astype(BF)
    far_v = jnp.stack([shifted(v, ROWS, i) for i in range(1, hops + 1)])
    qt, kt, near, prod, *saved = path_fwd(q, k, r, c, heads)
    far_k = jnp.stack([shifted(kt, ROWS, i) for i in range(1, hops + 1)])
    far_p = jnp.stack([shifted(prod, ROWS, i) for i in range(1, hops)])
    row_arr = jnp.full((1,), my_row, jnp.int32)
    attended, probs, chain = attn_fwd(lengths, row_arr, qt, near, v, far_k, far_v, far_p, heads, hops)

    attn_part = jnp.dot(attended, w_out, preferred_element_type=F32).astype(BF)
    attn_rows = lax.psum_scatter(attn_part, "wid", scatter_dimension=0, tiled=True)
    x_rows = lax.dynamic_slice_in_dim(x_all, my_wid * sub, sub, 0).astype(F32)
    dy_rows = lax.dynamic_slice_in_dim(dy_all, my_wid * sub, sub, 0).astype(F32)
    mixed = x_rows + attn_rows.astype(F32)
    normed_two, inverse_two = norm_rows(mixed)
    inner = lax.all_gather((normed_two * gain_two).astype(BF), "wid", axis=0, tiled=True)

    pre = jnp.einsum("tc,hcf->htf", inner, w_gu, preferred_element_type=F32)
    gate, up = pre[:, :, :ff], pre[:, :, ff:]
    sig = jax.nn.sigmoid(gate)
    hidden = (gate * sig * up).astype(BF)
    ffn_part = jnp.einsum("htf,hfc->tc", hidden, w_dn, preferred_element_type=F32)
    ffn_part = (ffn_part + attn_part.astype(F32)).astype(BF)
    ffn_cols = lax.psum_scatter(ffn_part, "wid", scatter_dimension=1, tiled=True)
    output = (inputs.astype(F32) + ffn_cols.astype(F32)).astype(BF)

    g_hidden = jnp.einsum("tc,hfc->htf", dy_all, w_dn, preferred_element_type=F32)
    g_gate = g_hidden * up * sig * (1.0 + gate * (1.0 - sig))
    g_up = g_hidden * gate * sig
    g_pre = jnp.concatenate([g_gate, g_up], 2).astype(BF)
    g_inner = jnp.einsum("htf,hcf->tc", g_pre, w_gu, preferred_element_type=F32).astype(BF)
    g_inner = lax.psum_scatter(g_inner, "wid", scatter_dimension=0, tiled=True).astype(F32)
    g_mixed_n, g_gain_two = norm_back(g_inner, normed_two, inverse_two, gain_two)
    g_z = lax.all_gather((dy_rows + g_mixed_n).astype(BF), "wid", axis=0, tiled=True)

    d_gu = jnp.einsum("tc,htf->hcf", inner, g_pre, preferred_element_type=F32).astype(BF)
    d_dn = jnp.einsum("htf,tc->hfc", hidden, dy_all, preferred_element_type=F32).astype(BF)
    d_gu = lax.psum_scatter(d_gu, "seq", scatter_dimension=1, tiled=True)
    d_gu = lax.psum_scatter(d_gu, "hid", scatter_dimension=0)
    d_dn = lax.psum_scatter(d_dn, "seq", scatter_dimension=2, tiled=True)
    d_dn = lax.psum_scatter(d_dn, "hid", scatter_dimension=0)

    g_attn = jnp.einsum("tc,ic->ti", g_z, w_out, preferred_element_type=F32).astype(BF)
    d_out = jnp.einsum("ti,tc->ic", attended, g_z, preferred_element_type=F32).astype(BF)
    g_qt, g_near, gv, send_k, send_v, send_p = attn_bwd(probs, g_attn, qt, v, far_v, far_p, chain, heads, hops)
    g_kt = sum(shifted(send_k[i - 1], ROWS, -i).astype(F32) for i in range(1, hops + 1))
    gv = gv + sum(shifted(send_v[i - 1], ROWS, -i).astype(F32) for i in range(1, hops + 1))
    g_prod = sum(shifted(send_p[i - 1], ROWS, -i).astype(F32) for i in range(1, hops))
    g_q, g_k, g_r, g_c = path_bwd(q, k, r, c, saved, g_qt, g_kt, g_near, g_prod, heads)
    g_v = gv.astype(BF)

    def weight_grad(grad_low):
        return jnp.einsum("tc,ti->ci", act, grad_low, preferred_element_type=F32).astype(BF)

    def input_grad(grad_low, weight):
        return jnp.einsum("ti,ci->tc", grad_low, weight, preferred_element_type=F32)

    g_act = (input_grad(g_q, w_query) + input_grad(g_k, w_key) + input_grad(g_v, w_value)
             + input_grad(g_r, w_house) + input_grad(g_c, w_beta))
    g_act = lax.psum_scatter(g_act.astype(BF), "wid", scatter_dimension=0, tiled=True).astype(F32)
    normed_rows = lax.dynamic_slice_in_dim(normed_one, my_wid * sub, sub, 0)
    inverse_rows = lax.dynamic_slice_in_dim(inverse_one, my_wid * sub, sub, 0)
    g_resid, g_gain_one = norm_back(g_act, normed_rows, inverse_rows, gain_one)
    d_rows = dy_rows + g_mixed_n + g_resid
    d_inputs = lax.all_to_all(d_rows, "wid", split_axis=1, concat_axis=0, tiled=True)

    def scatter(x, dim):
        return lax.psum_scatter(x, ROWS, scatter_dimension=dim, tiled=True)

    gains = lax.psum(jnp.stack([g_gain_one, g_gain_two]), "wid")
    gains = scatter(gains, 1)
    return (
        output,
        d_inputs,
        gains[0],
        gains[1],
        scatter(weight_grad(g_q), 0).astype(F32),
        scatter(weight_grad(g_k), 0).astype(F32),
        scatter(weight_grad(g_v), 0).astype(F32),
        scatter(weight_grad(g_r), 0).astype(F32),
        scatter(weight_grad(g_c), 0).astype(F32),
        scatter(d_out, 1).astype(F32),
        d_gu[:, :ff].astype(F32),
        d_gu[:, ff:].astype(F32),
        d_dn.astype(F32),
    )


def fast_body(inputs, gain_attn, gain_ffn, w_query, w_key, w_value, w_house, w_beta, w_out,
              w_gate, w_up, w_down, lengths, cotangent):
    tok, col = inputs.shape
    row_devs = lax.axis_size(ROWS)
    sizes = tuple(lax.axis_size(i) for i in ("seq", "hid", "wid"))
    most_len = max(LEAST, 2 * tok * row_devs // 5)
    hops = min((most_len - 2) // tok + 1, row_devs - 1)
    heads = w_query.shape[1] // HDIM
    f = step((lengths, inputs, cotangent, gain_attn, gain_ffn, w_query, w_key, w_value, w_house,
              w_beta.T, w_out, w_gate, w_up, w_down), heads, hops, sizes)
    names = [i for i in f if i != "gain_out"]
    f.update(zip(names, finish([f[i] for i in names])))
    return (f["output"], f["d_inputs"], f["gain_out"][0], f["gain_out"][1], f["d_query"], f["d_key"], f["d_value"],
            f["d_house"], f["d_beta"].T, f["d_out"].T, f["d_gate"], f["d_up"], f["d_down"])


def slow(mesh):
    return (mesh.shape["seq"], mesh.shape["hid"]) != (2, 4)


def solution(mesh):
    in_specs = (
        P(("seq", "hid"), "wid"), P("wid"), P("wid"),
        P(None, "wid"), P(None, "wid"), P(None, "wid"), P(None, "wid"), P(None, "wid"),
        P("wid", None), P(None, ("hid", "wid")), P(None, ("hid", "wid")), P(("hid", "wid"), None),
        P(), P(("seq", "hid"), "wid"),
    )
    out_specs = (
        P(("seq", "hid"), "wid"), P(("seq", "hid"), "wid"), P(("seq", "hid")), P(("seq", "hid")),
        P(("seq", "hid"), "wid"), P(("seq", "hid"), "wid"), P(("seq", "hid"), "wid"),
        P(("seq", "hid"), "wid"), P(("seq", "hid"), "wid"), P("wid", ("seq", "hid")),
        P("seq", ("hid", "wid")), P("seq", ("hid", "wid")), P(("hid", "wid"), "seq"),
    )
    return jax.shard_map(body if slow(mesh) else fast_body, mesh=mesh, in_specs=in_specs, out_specs=out_specs, check_vma=False)
```

profile of v0, /device:TPU:0, one launch (start us, length us, event | category | flops | bytes accessed | tf_op | source)
XLA Modules:
  0.0 215.8 jit_solution(14472252332960161235)
XLA Ops:
  0.7 209.5 %step.1 = (bf16[256,384]{1,0:T(8,128)(2,1)}, f32[256,384]{1,0:T(8,128)}, f32[8,192]{1,0:T(8,128)}, f32[192,384]{1,0:T(8,128)}, f32[192,384]{1,0:T(8,128)}, /*ind...) custom-call(s32[3]{0:T(128)} %refs_0_.1, ...), custom_call_target="tpu_custom_call" | custom-call | tf_op jit(solution)/shard_map/step/pallas_call | solution.py:948
  210.2 4.2 %finish.1 = (bf16[256,384]{1,0:T(8,128)(2,1)}, f32[256,384]{1,0:T(8,128)}, f32[192,384]{1,0:T(8,128)}, f32[192,384]{1,0:T(8,128)}, f32[192,384]{1,0:T(8,128)}, /...) custom-call(bf16[256,384]{1,0:T(8,128)(2,1)} %get-tuple-element.36.r, ...), custom_call_target="tpu_custom_call" | custom-call | tf_op jit(solution)/shard_map/finish/pallas_call | solution.py:977
  214.4 1.3 fusion
where the time goes:
time: 216 us
  Pallas kernels  214 us (99%)
    pallas_call x1, Pallas kernels, step(): pl.pallas_call(functools.partial(step_kernel, (heads, hops, sizes), ins +...  210 us

commit v1 on v0

--- a/solution.py
+++ b/solution.py
@@ -59,29 +59,30 @@
     n = c_ref.shape[0]
     rows, cols = iotas(n)
     strength = c_ref[...]
-    us, us2, lows, invs = [], [], [], []
+    us2 = []
     for h in range(heads):
         raw = r_ref[:, head_cols(h)]
         inv, root = house_terms(raw, strength, heads, h)
         u = raw * (inv * root)
         u_ref[:, head_cols(h)] = u
         u2 = split(u)
+        us2.append(u2)
         low = jnp.where(rows > cols, dot3(u2, u2, 1, 1), 0.0)
-        us.append(u)
-        us2.append(u2)
-        lows.append(low)
-        first = jnp.where(rows == cols, 1.0, 0.0) - jnp.where(rows // 2 == cols // 2, low, 0.0)
-        invs.append(first)
-    span = 2
-    while span < n:
-        pick = (rows // (2 * span) == cols // (2 * span)) & (rows // span != cols // span)
-        halves = [split(m) for m in invs]
-        mids = [dot3(split(jnp.where(pick, lows[h], 0.0)), halves[h], 1, 0) for h in range(heads)]
-        invs = [invs[h] - dot3(halves[h], split(mids[h]), 1, 0) for h in range(heads)]
-        span = span * 2
+        psi_ref[h] = low
+        inv_ref[h] = jnp.where(rows == cols, 1.0, 0.0) - jnp.where(rows // 2 == cols // 2, low, 0.0)
+
+    def double(step, carry):
+        apart = jnp.right_shift(rows, step) != jnp.right_shift(cols, step)
+        pick = apart & (jnp.right_shift(rows, step + 1) == jnp.right_shift(cols, step + 1))
+        halves = [split(inv_ref[h]) for h in range(heads)]
+        mids = [dot3(split(jnp.where(pick, psi_ref[h], 0.0)), halves[h], 1, 0) for h in range(heads)]
+        for h in range(heads):
+            inv_ref[h] = inv_ref[h] - dot3(halves[h], split(mids[h]), 1, 0)
+        return carry
+
+    lax.fori_loop(1, (n - 1).bit_length(), double, 0)
     for h in range(heads):
-        inv_ref[h] = invs[h]
-        kin = split(invs[h])
+        kin = split(inv_ref[h])
         q = q_ref[:, head_cols(h)]
         k = k_ref[:, head_cols(h)]
         q2, k2, u2 = split(q), split(k), us2[h]
@@ -136,52 +137,56 @@
     return r * (r - 1) // 2 + m
 
 
-def attn_fwd_stage(heads, hops, row, len_ref, qt_ref, near_ref, v_ref, fv_ref, fp_ref, chain_ref,
-                   o_ref, p_ref, s_ref, get_k, get_p):
+def key_chain(hops, h, fp_ref, chain_ref):
+    cs = head_cols(h)
+    for r in range(2, hops + 1):
+        keys = chain_ref[chain_slot(r, 0), :, cs]
+        for m in range(1, r):
+            keys = dot(keys, fp_ref[r - m - 1, h].astype(BF), 1, 1).astype(BF)
+            chain_ref[chain_slot(r, m), :, cs] = keys
+
+
+def attn_fwd_rows(hops, h, start, count, row, len_ref, qt_ref, near_ref, v_ref, fv_ref, chain_ref,
+                  o_ref, p_ref, rcp_ref, s_ref):
     n = qt_ref.shape[0]
     scale = HDIM ** (-0.5)
-    rows, cols = iotas(n)
+    cs, rs = head_cols(h), slice(start, start + count)
+    rows = start + lax.broadcasted_iota(jnp.int32, (count, n), 0)
+    cols = lax.broadcasted_iota(jnp.int32, (count, n), 1)
     own = doc_of(row * n + rows, len_ref)
     near_ok = (rows >= cols) & (own == doc_of(row * n + cols, len_ref))
-    for h in range(heads):
-        cs = head_cols(h)
-        q = qt_ref[:, cs]
-        for copy in get_k[h] + get_p[h]:
-            copy.wait_recv()
-        s = jnp.where(near_ok, near_ref[h] * scale, neg_big)
-        s_ref[0:n, :] = s
-        top = jnp.max(s, 1, keepdims=True)
-        for r in range(1, hops + 1):
-            keys = chain_ref[chain_slot(r, 0), :, cs]
-            for m in range(1, r):
-                keys = dot(keys, fp_ref[r - m - 1, h].astype(BF), 1, 1).astype(BF)
-                chain_ref[chain_slot(r, m), :, cs] = keys
-            source = row - r
-            docs = jnp.where(source >= 0, doc_of(source * n + cols, len_ref), -1)
-            s = jnp.where(own == docs, dot(q, keys, 1, 1) * scale, neg_big)
-            s_ref[r * n:(r + 1) * n, :] = s
-            top = jnp.maximum(top, jnp.max(s, 1, keepdims=True))
-        total = jnp.zeros((n, 1), F32)
-        for r in range(hops + 1):
-            e = jnp.exp(s_ref[r * n:(r + 1) * n, :] - top)
-            s_ref[r * n:(r + 1) * n, :] = e
-            total = total + jnp.sum(e, 1, keepdims=True)
-        recip = 1.0 / total
-        out = jnp.zeros((n, HDIM), F32)
-        for r in range(hops + 1):
-            p = (s_ref[r * n:(r + 1) * n, :] * recip).astype(BF)
-            p_ref[r, h] = p
-            vals = v_ref[:, cs] if r == 0 else fv_ref[r - 1, :, cs]
-            out = out + dot(p, vals, 1, 0)
-        o_ref[:, cs] = out.astype(BF)
+    q = qt_ref[rs, cs]
+    s = jnp.where(near_ok, near_ref[h, rs, :] * scale, neg_big)
+    s_ref[0:count, :] = s
+    top = jnp.max(s, 1, keepdims=True)
+    for r in range(1, hops + 1):
+        source = row - r
+        docs = jnp.where(source >= 0, doc_of(source * n + cols, len_ref), -1)
+        keys = chain_ref[chain_slot(r, r - 1), :, cs]
+        s = jnp.where(own == docs, dot(q, keys, 1, 1) * scale, neg_big)
+        s_ref[r * count:(r + 1) * count, :] = s
+        top = jnp.maximum(top, jnp.max(s, 1, keepdims=True))
+    total = jnp.zeros((count, 1), F32)
+    out = jnp.zeros((count, HDIM), F32)
+    for r in range(hops + 1):
+        e = jnp.exp(s_ref[r * count:(r + 1) * count, :] - top)
+        total = total + jnp.sum(e, 1, keepdims=True)
+        weights = e.astype(BF)
+        p_ref[r, h, rs, :] = weights
+        out = out + dot(weights, v_ref[:, cs] if r == 0 else fv_ref[r - 1, :, cs], 1, 0)
+    recip = 1.0 / total
+    rcp_ref[rs, h:h + 1] = recip
+    o_ref[rs, cs] = (out * recip).astype(BF)
+
 
 def attn_fwd_kernel(heads, hops, len_ref, row_ref, qt_ref, near_ref, v_ref, fk_ref, fv_ref, fp_ref,
-                    o_ref, p_ref, chain_ref, s_ref):
+                    o_ref, p_ref, chain_ref, rcp_ref, s_ref):
     for r in range(1, hops + 1):
         chain_ref[chain_slot(r, 0)] = fk_ref[r - 1]
-    none = [[] for _ in range(heads)]
-    attn_fwd_stage(heads, hops, row_ref[0], len_ref, qt_ref, near_ref, v_ref, fv_ref, fp_ref, chain_ref,
-                   o_ref, p_ref, s_ref, none, none)
+    for h in range(heads):
+        key_chain(hops, h, fp_ref, chain_ref)
+        attn_fwd_rows(hops, h, 0, qt_ref.shape[0], row_ref[0], len_ref, qt_ref, near_ref, v_ref, fv_ref, chain_ref,
+                      o_ref, p_ref, rcp_ref, s_ref)
 
 
 def attn_fwd(lengths, my_row, qt, near, v, far_k, far_v, far_p, heads, hops):
@@ -196,6 +201,7 @@
             jax.ShapeDtypeStruct((n, width), BF),
             jax.ShapeDtypeStruct((hops + 1, heads, n, n), BF),
             jax.ShapeDtypeStruct((slots, n, width), BF),
+            jax.ShapeDtypeStruct((n, heads), F32),
         ),
         scratch_shapes=[pltpu.VMEM(((hops + 1) * n, n), F32)],
         compiler_params=pltpu.CompilerParams(vmem_limit_bytes=VMEM_LIMIT),
@@ -203,44 +209,14 @@
     )(lengths, my_row, qt, near, v, far_k, far_v, far_p)
 
 
-def attn_bwd_kernel(heads, hops, p_ref, go_ref, qt_ref, v_ref, fv_ref, fp_ref, chain_ref,
+def attn_bwd_kernel(heads, hops, p_ref, rcp_ref, go_ref, qt_ref, v_ref, fv_ref, fp_ref, chain_ref,
                     gqt_ref, gnear_ref, gv_ref, sendk_ref, sendv_ref, sendp_ref, dp_ref):
-    n = qt_ref.shape[0]
-    scale = HDIM ** (-0.5)
     for h in range(heads):
-        cs = head_cols(h)
-        go = go_ref[:, cs]
-        q = qt_ref[:, cs]
-        delta = jnp.zeros((n, 1), F32)
-        for r in range(hops + 1):
-            vals = v_ref[:, cs] if r == 0 else fv_ref[r - 1, :, cs]
-            dp = dot(go, vals, 1, 1)
-            dp_ref[r] = dp
-            delta = delta + jnp.sum(p_ref[r, h].astype(F32) * dp, 1, keepdims=True)
-            gv = dot(p_ref[r, h], go, 0, 0)
-            if r == 0:
-                gv_ref[:, cs] = gv
-            else:
-                sendv_ref[r - 1, :, cs] = gv.astype(BF)
-        gnear_ref[h] = p_ref[0, h].astype(F32) * (dp_ref[0] - delta) * scale
-        gq = jnp.zeros((n, HDIM), F32)
-        gps = [jnp.zeros((HDIM, HDIM), F32) for _ in range(hops - 1)]
-        for r in range(1, hops + 1):
-            gs = (p_ref[r, h].astype(F32) * (dp_ref[r] - delta) * scale).astype(BF)
-            gq = gq + dot(gs, chain_ref[chain_slot(r, r - 1), :, cs], 1, 0)
-            gk = dot(gs, q, 0, 0)
-            for m in range(r - 1, 0, -1):
-                back = r - m - 1
-                gkb = gk.astype(BF)
-                gps[back] = gps[back] + dot(gkb, chain_ref[chain_slot(r, m - 1), :, cs], 0, 0)
-                gk = dot(gkb, fp_ref[back, h].astype(BF), 1, 0)
-            sendk_ref[r - 1, :, cs] = gk.astype(BF)
-        gqt_ref[:, cs] = gq
-        for i in range(hops - 1):
-            sendp_ref[i, h] = gps[i].astype(BF)
-
-
-def attn_bwd(p, go, qt, v, far_v, far_p, chain, heads, hops):
+        attn_bwd_head(hops, h, p_ref, rcp_ref, go_ref[:, head_cols(h)], qt_ref, v_ref, fv_ref, fp_ref, chain_ref,
+                      gqt_ref, gnear_ref, gv_ref, sendk_ref, sendv_ref, sendp_ref, dp_ref)
+
+
+def attn_bwd(p, rcp, go, qt, v, far_v, far_p, chain, heads, hops):
     n, width = qt.shape
     return pl.pallas_call(
         functools.partial(attn_bwd_kernel, heads, hops),
@@ -252,59 +228,23 @@
             jax.ShapeDtypeStruct((hops, n, width), BF),
             jax.ShapeDtypeStruct((hops - 1, heads, HDIM, HDIM), BF),
         ),
-        scratch_shapes=[pltpu.VMEM((hops + 1, n, n), F32)],
+        scratch_shapes=[pltpu.VMEM(((hops + 1) * n, n), F32)],
         compiler_params=pltpu.CompilerParams(vmem_limit_bytes=VMEM_LIMIT),
         name="attn_bwd",
-    )(p, go, qt, v, far_v, far_p, chain)
+    )(p, rcp, go, qt, v, far_v, far_p, chain)
 
 
 def path_bwd_kernel(heads, q_ref, k_ref, r_ref, c_ref, u_ref, inv_ref, psi_ref, x_ref, y_ref,
                     gqt_ref, gkt_ref, gnear_ref, gp_ref, gq_ref, gk_ref, gr_ref, gc_ref):
-    n = q_ref.shape[0]
-    rows, cols = iotas(n)
-    strength = c_ref[...]
-    lane = lax.broadcasted_iota(jnp.int32, strength.shape, 1)
-    gc_all = jnp.zeros(strength.shape, F32)
+    lane = lax.broadcasted_iota(jnp.int32, c_ref.shape, 1)
+    gc_all = jnp.zeros(c_ref.shape, F32)
     for h in range(heads):
         cs = head_cols(h)
-        q, k, u = q_ref[:, cs], k_ref[:, cs], u_ref[:, cs]
-        qb, kb, ub = q.astype(BF), k.astype(BF), u.astype(BF)
-        kin = inv_ref[h].astype(BF)
-        psi = psi_ref[h].astype(BF)
-        x, y = x_ref[:, cs].astype(BF), y_ref[:, cs].astype(BF)
-        gqt, gkt = gqt_ref[:, cs], gkt_ref[:, cs]
-        gqtb, gktb = gqt.astype(BF), gkt.astype(BF)
-        gs = gnear_ref[h]
-        gsb = gs.astype(BF)
-        gst = gs.T.astype(BF)
-        gp = gp_ref[h].astype(BF)
-        f = jnp.where(rows <= cols, dot(ub, qb, 1, 1), 0.0).astype(BF)
-        fq = jnp.where(rows >= cols, dot(qb, ub, 1, 1), 0.0).astype(BF)
-        a = jnp.where(rows > cols, dot(ub, kb, 1, 1), 0.0).astype(BF)
-        gx = -(dot(f, gqtb, 1, 0) + dot(ub, gp, 1, 0))
-        gy = -dot(a, gktb, 1, 0)
-        phiq = dot(fq, kin, 1, 0).astype(BF)
-        back = dot(gst, phiq, 1, 0)
-        backb = back.astype(BF)
-        gfq = jnp.where(rows >= cols, -(dot(gqtb, x, 1, 1) + dot(gsb, psi, 1, 1)), 0.0)
-        gaq = jnp.where(rows < cols, -(dot(gktb, y, 1, 1) + back), 0.0)
-        kgx = dot(kin, gx.astype(BF), 0, 0)
-        kgy = dot(kin, gy.astype(BF), 1, 0)
-        zt = dot(x, kgx.astype(BF), 1, 1) + dot(kgy.astype(BF), y, 1, 1) - dot(psi, backb, 1, 0)
-        glt = jnp.where(rows < cols, -zt, 0.0)
-        sym = (glt + glt.T).astype(BF)
-        gfqb, gaqb = gfq.astype(BF), gaq.astype(BF)
-        gu = (kgx + kgy - dot(x, gp, 1, 1) + dot(gfq.T.astype(BF), qb, 1, 0)
-              + dot(gaq.T.astype(BF), kb, 1, 0) + dot(sym, ub, 1, 0))
-        gq_ref[:, cs] = (gqt + dot(gsb, kb, 1, 0) + dot(gfqb, ub, 1, 0)).astype(BF)
-        gk_ref[:, cs] = (gkt + dot(gst, qb, 1, 0) + dot(gaqb, ub, 1, 0)).astype(BF)
-        raw = r_ref[:, cs]
-        inv, root = house_terms(raw, strength, heads, h)
-        gc = jnp.sum(gu * u, 1, keepdims=True) * (1.0 - 0.5 * root * root) * 0.5
-        gun = gu * root
-        un = raw * inv
-        gr = inv * (gun - un * jnp.sum(gun * un, 1, keepdims=True))
-        gr_ref[:, cs] = gr.astype(BF)
+        gq, gk, gr, gc = path_bwd_head(h, heads, q_ref, k_ref, r_ref, c_ref, u_ref, inv_ref, psi_ref, x_ref, y_ref,
+                                       gqt_ref[:, cs], gkt_ref[:, cs], gnear_ref[h], gp_ref[h])
+        gq_ref[:, cs] = gq
+        gk_ref[:, cs] = gk
+        gr_ref[:, cs] = gr
         gc_all = jnp.where(lane == h, gc, gc_all)
     gc_ref[...] = gc_all.astype(BF)
 
@@ -327,15 +267,23 @@
     def __init__(self, send, recv):
         self.send, self.recv, self.count, self.open = send, recv, 0, []
 
-    def start(self, src, dst, device):
-        i = self.count
-        self.count = i + 1
-        copy = pltpu.make_async_remote_copy(
-            src_ref=src, dst_ref=dst, send_sem=self.send.at[i], recv_sem=self.recv.at[i],
+    def take(self):
+        self.count = self.count + 1
+        return self.count - 1
+
+    def make(self, src, dst, device, send, recv):
+        return pltpu.make_async_remote_copy(
+            src_ref=src, dst_ref=dst, send_sem=self.send.at[send], recv_sem=self.recv.at[recv],
             device_id=device, device_id_type=MESH)
+
+    def begin(self, copy):
         copy.start()
         self.open.append(copy)
         return copy
+
+    def start(self, src, dst, device):
+        i = self.take()
+        return self.begin(self.make(src, dst, device, i, i))
 
     def sent(self, some):
         for copy in some:
@@ -385,32 +333,137 @@
         pl.semaphore_wait(sem, self.wid_n - 1 + self.rows_n - 1)
 
 
+class Sometimes:
+    def __init__(self, copy, sends=None, gets=None):
+        self.copy, self.sends, self.gets = copy, sends, gets
+
+    def on(self, flag, act):
+        if flag is None:
+            act()
+        else:
+            pl.when(flag)(act)
+
+    def start(self):
+        self.on(self.sends, lambda: self.copy.start() and None)
+
+    def wait_send(self):
+        self.on(self.sends, self.copy.wait_send)
+
+    def wait_recv(self):
+        self.on(self.gets, self.copy.wait_recv)
+
+
+class LineGather:
+    def __init__(self, copies, place, src, view):
+        me = place.wid
+        self.me, self.copies, self.view = me, copies, view
+        self.ids = [copies.take() for _ in range(3)]
+        here = view(me)
+        self.by = {i: copies.make(src, here, {"wid": place.wid_peer(i)}, self.ids[i - 1], self.ids[i - 1])
+                   for i in (1, 2, 3)}
+        self.by[1] = Sometimes(self.by[1], me != 3)
+        self.by[3] = Sometimes(self.by[3], me != 0)
+        for i in (2, 1, 3):
+            copies.begin(self.by[i])
+
+    def relay(self):
+        self.by[2].wait_recv()
+        for m, chunk, to, i in ((1, 3, 0, 1), (2, 0, 3, 3)):
+            part = self.view(chunk)
+            copy = self.copies.make(part, part, {"wid": to}, self.copies.take(), self.ids[i - 1])
+            self.copies.begin(Sometimes(copy, self.me == m))
+
+    def wait(self):
+        self.by[1].wait_recv()
+        self.by[3].wait_recv()
+
+
+class LineSwap:
+    def __init__(self, copies, place, piece, recv):
+        self.copies, self.place, self.me, self.piece, self.recv = copies, place, place.wid, piece, recv
+        self.ids = [copies.take() for _ in range(4)]
+        me = self.me
+
+        @pl.when(me == 0)
+        def _():
+            recv(0)[...] = jnp.zeros(recv(0).shape, BF)
+
+        @pl.when(me == 3)
+        def _():
+            recv(2)[...] = jnp.zeros(recv(2).shape, BF)
+
+    def make(self, src, i, slot, device, send):
+        return self.copies.make(src, self.recv(slot), device, send, self.ids[slot])
+
+    def start_far(self):
+        self.far = []
+        for end, far, middle in ((0, 3, 1), (3, 0, 2)):
+            copy = Sometimes(self.make(self.piece(far), 0, 3, {"wid": middle}, self.copies.take()),
+                             self.me == end, self.me == middle)
+            self.copies.begin(copy)
+            self.far.append(copy)
+
+    def start(self):
+        me, place = self.me, self.place
+        to = [place.wid_peer(i) for i in range(4)]
+        self.two = Sometimes(self.make(self.piece(to[2]), 2, 1, {"wid": to[2]}, self.ids[1]), (me == 0) | (me == 3))
+        self.one = Sometimes(self.make(self.piece(to[1]), 1, 0, {"wid": to[1]}, self.ids[0]), me != 3, me != 0)
+        self.three = Sometimes(self.make(self.piece(to[3]), 3, 2, {"wid": to[3]}, self.ids[2]), me != 0, me != 3)
+        for copy in (self.two, self.one, self.three):
+            self.copies.begin(copy)
+
+    def combine(self):
+        for copy in self.far:
+            copy.wait_recv()
+        mid = (self.me == 1) | (self.me == 2)
+        far = 3 * (2 - jnp.minimum(jnp.maximum(self.me, 1), 2))
+
+        @pl.when(mid)
+        def _():
+            at = self.recv(3)
+            at[...] = (at[...].astype(F32) + self.piece(far)[...].astype(F32)).astype(BF)
+
+        copy = self.make(self.recv(3), 2, 1, {"wid": far}, self.copies.take())
+        self.copies.begin(Sometimes(copy, mid))
+
+    def total(self, own):
+        for copy in (self.two, self.one, self.three):
+            copy.wait_recv()
+        for slot in range(3):
+            own = own + self.recv(slot)[...].astype(F32)
+        return own
+
+
 def aligned(start, size, step):
     return pl.ds(pl.multiple_of(start, step), size)
 
 
-def attn_bwd_head(hops, h, p_ref, go, qt_ref, v_ref, fv_ref, fp_ref, chain_ref,
+def attn_bwd_head(hops, h, p_ref, rcp_ref, go, qt_ref, v_ref, fv_ref, fp_ref, chain_ref,
                   gqt_ref, gnear_ref, gv_ref, sendk_ref, sendv_ref, sendp_ref, dp_ref):
     n = qt_ref.shape[0]
     scale = HDIM ** (-0.5)
     cs = head_cols(h)
     q = qt_ref[:, cs]
+    recip = rcp_ref[:, h:h + 1]
+    go_low = (go.astype(F32) * recip).astype(BF)
     delta = jnp.zeros((n, 1), F32)
     for r in range(hops + 1):
         vals = v_ref[:, cs] if r == 0 else fv_ref[r - 1, :, cs]
         dp = dot(go, vals, 1, 1)
         dp_ref[r * n:(r + 1) * n, :] = dp
         delta = delta + jnp.sum(p_ref[r, h].astype(F32) * dp, 1, keepdims=True)
-        gv = dot(p_ref[r, h], go, 0, 0)
+        gv = dot(p_ref[r, h], go_low, 0, 0)
         if r == 0:
             gv_ref[:, cs] = gv
         else:
             sendv_ref[r - 1, :, cs] = gv.astype(BF)
-    gnear_ref[h] = p_ref[0, h].astype(F32) * (dp_ref[0:n, :] - delta) * scale
+    delta = delta * recip
+    factor = recip * scale
+    gnear_ref[h] = p_ref[0, h].astype(F32) * ((dp_ref[0:n, :] - delta) * factor)
     gq = jnp.zeros((n, HDIM), F32)
     gps = [jnp.zeros((HDIM, HDIM), F32) for _ in range(hops - 1)]
     for r in range(1, hops + 1):
-        gs = (p_ref[r, h].astype(F32) * (dp_ref[r * n:(r + 1) * n, :] - delta) * scale).astype(BF)
+        gs = (p_ref[r, h].astype(F32) * ((dp_ref[r * n:(r + 1) * n, :] - delta) * factor)).astype(BF)
         gq = gq + dot(gs, chain_ref[chain_slot(r, r - 1), :, cs], 1, 0)
         gk = dot(gs, q, 0, 0)
         for m in range(r - 1, 0, -1):
@@ -496,7 +549,18 @@
     piece = model // place.rows_n
     copies, loads = Copies(R.send_sem, R.recv_sem), Loads(R.load_sem)
     my_cols = aligned(place.wid * col, col, 128)
-    my_rows = aligned(place.wid * sub, sub, sub)
+    part_n = n // 2
+    step_n = sub // 2
+
+    def rows_of(w, hh):
+        return aligned(hh * part_n + w * step_n, step_n, step_n)
+
+    def half_of(hh):
+        return slice(hh * step_n, (hh + 1) * step_n)
+
+    def own_rows(ref):
+        return jnp.concatenate([ref[rows_of(place.wid, hh), :].astype(F32) for hh in range(2)], 0)
+
     mine = aligned(place.seq * half, half, 128)
     other = aligned((1 - place.seq) * half, half, 128)
     sibling = {"seq": 1 - place.seq}
@@ -504,7 +568,31 @@
     to_wid = [{"wid": place.wid_peer(i)} for i in order]
     near = [{"hid": turned(place.hid, j)} for j in range(hid_n)]
 
-    load_x = [loads.start(R.x, R.xall.at[:, my_cols])]
+    R.gain_in[0:1, :] = R.gain_attn[...].astype(F32).reshape(1, col)
+    R.gain_in[1:2, :] = R.gain_ffn[...].astype(F32).reshape(1, col)
+    R.xall[:, my_cols] = R.x[...]
+    R.gall[:, my_cols] = R.gain_in[...]
+    place.barrier()
+
+    get_x = LineGather(copies, place, R.x, lambda c: R.xall.at[:, aligned(c * col, col, 128)])
+    get_gains = [copies.start(R.gain_in, R.gall.at[:, my_cols], d) for d in to_wid]
+
+    part_f = ff // seq_n
+    mine_c = aligned(place.seq * half, half, 16)
+    mine_f = aligned(place.seq * part_f, part_f, 16)
+
+    def cols_of(j):
+        return pl.ds(j * ff, ff)
+
+    def down_rows(j, piece_i=0, pieces=1):
+        size = part_f // pieces
+        return aligned(j * ff + place.seq * part_f + piece_i * size, size, 16)
+
+    def pass_on(ref, device):
+        return copies.start(ref, ref, device)
+
+    get_gate = [copies.start(R.wg.at[mine_c, :], R.wg_s.at[mine_c, cols_of(j)], near[j]) for j in (1, 2)]
+    get_up = [copies.start(R.wu.at[mine_c, :], R.wu_s.at[mine_c, cols_of(j)], near[j]) for j in (1, 2)]
     load_v = loads.start(R.wv, R.w_s.at[:, pl.ds(3 * width, width)])
     load_w = [loads.start(w.at[:, pl.ds(h * HDIM, HDIM)], R.w_s.at[:, pl.ds((3 * h + m) * HDIM, HDIM)])
               for h in range(heads) for m, w in enumerate((R.wq, R.wk, R.wr))]
@@ -512,36 +600,10 @@
     load_o = loads.start(R.wo, R.wo_s)
     load_f = [loads.start(R.wg, R.wg_s.at[:, pl.ds(0, ff)]), loads.start(R.wu, R.wu_s.at[:, pl.ds(0, ff)]),
               loads.start(R.wd, R.wd_s.at[pl.ds(0, ff), :])]
-    R.gain_in[0:1, :] = R.gain_attn[...].astype(F32).reshape(1, col)
-    R.gain_in[1:2, :] = R.gain_ffn[...].astype(F32).reshape(1, col)
-    place.barrier()
-
-    get_x = [copies.start(R.x, R.xall.at[:, my_cols], d) for d in to_wid]
-    get_x += [copies.start(R.gain_in, R.gall.at[:, my_cols], d) for d in to_wid]
-    R.gall[:, my_cols] = R.gain_in[...]
-
-    part_f = ff // seq_n
-    mine_c = aligned(place.seq * half, half, 16)
-    mine_f = aligned(place.seq * part_f, part_f, 16)
-
-    def cols_of(j):
-        return pl.ds(j * ff, ff)
-
-    def down_rows(j, piece_i=0, pieces=1):
-        size = part_f // pieces
-        return aligned(j * ff + place.seq * part_f + piece_i * size, size, 16)
-
-    def pass_on(ref, device):
-        return copies.start(ref, ref, device)
-
-    get_gate = [copies.start(R.wg.at[mine_c, :], R.wg_s.at[mine_c, cols_of(j)], near[j]) for j in (1, 2)]
-    for copy in get_gate:
-        copy.wait_recv()
-    get_gate3 = copies.start(R.wg_s.at[mine_c, cols_of(1)], R.wg_s.at[mine_c, cols_of(3)], near[2])
-
-    for copy in load_x:
-        copy.wait()
-    for copy in get_x:
+
+    get_x.relay()
+    get_x.wait()
+    for copy in get_gains:
         copy.wait_recv()
     get_dy = [copies.start(R.dy, R.dyall.at[:, my_cols], d) for d in to_wid]
     xf = R.xall[...].astype(F32)
@@ -569,50 +631,70 @@
     path_fwd_stage(heads, Heads(R.proj, 0), Heads(R.proj, 1), Heads(R.proj, 2), R.c, R.qt, R.kt_s, R.near_s, R.prod_s,
                    R.u, R.inv, R.psi, R.x1, R.y1, send_head)
 
-    get_up = [copies.start(R.wu.at[mine_c, :], R.wu_s.at[mine_c, cols_of(j)], near[j]) for j in (1, 2)]
+    for copy in get_gate + get_up:
+        copy.wait_recv()
+    relay = [copies.start(R.wg_s.at[mine_c, cols_of(1)], R.wg_s.at[mine_c, cols_of(3)], near[2]),
+             copies.start(R.wu_s.at[mine_c, cols_of(2)], R.wu_s.at[mine_c, cols_of(3)], near[1])]
     get_down = [copies.start(R.wd.at[mine_f, :], R.wd_s.at[down_rows(j), :], near[j]) for j in (1, 2)]
 
     for copy in get_v:
         copy.wait_recv()
-    attn_fwd_stage(heads, hops, place.row, R.lengths, R.qt, R.near_s, R.v, R.fv, R.fp, R.chain,
-                   R.o, R.probs, R.s_s, get_k, get_p)
-
     load_o.wait()
     get_a = []
-    for slot, i in enumerate(order):
-        peer = place.wid_peer(i)
-        rows = aligned(peer * sub, sub, sub)
-        R.part_s[rows, :] = dot(R.o[rows, :], R.wo_s[...], 1, 0).astype(BF)
-        get_a.append(copies.start(R.part_s.at[rows, :], R.recv_s.at[slot], {"wid": peer}))
-    R.part_s[my_rows, :] = dot(R.o[my_rows, :], R.wo_s[...], 1, 0).astype(BF)
-    for copy in get_up + get_down:
-        copy.wait_recv()
-    relay = [copies.start(R.wu_s.at[mine_c, cols_of(2)], R.wu_s.at[mine_c, cols_of(3)], near[1]),
-             copies.start(R.wd_s.at[down_rows(1, 0, 2), :], R.wd_s.at[down_rows(3, 0, 2), :], near[2]),
-             copies.start(R.wd_s.at[down_rows(2, 1, 2), :], R.wd_s.at[down_rows(3, 1, 2), :], near[1])]
-    get_gate3.wait_recv()
+    for hh in range(2):
+        for h in range(heads):
+            if hh == 0:
+                for copy in get_k[h] + get_p[h]:
+                    copy.wait_recv()
+                key_chain(hops, h, R.fp, R.chain)
+            attn_fwd_rows(hops, h, hh * part_n, part_n, place.row, R.lengths, R.qt, R.near_s, R.v, R.fv, R.chain,
+                          R.o, R.probs, R.rcp, R.s_s)
+        rs = slice(hh * part_n, (hh + 1) * part_n)
+        R.part_s[rs, :] = dot(R.o[rs, :], R.wo_s[...], 1, 0).astype(BF)
+        get_a.append(LineSwap(copies, place, functools.partial(lambda hh, c: R.part_s.at[rows_of(c, hh), :], hh),
+                              functools.partial(lambda hh, q: R.recv_s.at[q, pl.ds(hh * step_n, step_n), :], hh)))
+        get_a[hh].start_far()
+        get_a[hh].start()
     three = pl.ds(ff, 3 * ff)
-    shared = [pass_on(R.wg_s.at[mine_c, three], sibling)]
-    mixed = R.xall[my_rows, :].astype(F32) + R.part_s[my_rows, :].astype(F32)
-    for slot, copy in enumerate(get_a):
-        copy.wait_recv()
-        mixed = mixed + R.recv_s[slot].astype(F32)
-    R.mixed[...] = mixed
-    inv_two = lax.rsqrt(jnp.mean(mixed * mixed, -1, keepdims=True) + eps_norm)
-    R.row_s[...] = (mixed * inv_two * R.gall[1:2, :]).astype(BF)
-    get_i = [copies.start(R.row_s, R.inner.at[my_rows, :], d) for d in to_wid]
-    R.inner[my_rows, :] = R.row_s[...]
+    get_i = []
+
+    def mix(hh):
+        at, keep = rows_of(place.wid, hh), half_of(hh)
+        mixed = get_a[hh].total(R.xall[at, :].astype(F32) + R.part_s[at, :].astype(F32))
+        R.mixed[keep, :] = mixed
+        inv_two = lax.rsqrt(jnp.mean(mixed * mixed, -1, keepdims=True) + eps_norm)
+        R.row_s[keep, :] = (mixed * inv_two * R.gall[1:2, :]).astype(BF)
+        get_i.append(LineGather(copies, place, R.row_s.at[pl.ds(hh * step_n, step_n), :],
+                                functools.partial(lambda hh, c: R.inner.at[rows_of(c, hh), :], hh)))
+        R.inner[at, :] = R.row_s[keep, :]
+
+    get_a[0].combine()
+    mix(0)
+    get_a[1].combine()
     for copy in relay:
         copy.wait_recv()
-    shared.append(pass_on(R.wu_s.at[mine_c, three], sibling))
+    shared = [pass_on(ref.at[mine_c, three], sibling) for ref in (R.wg_s, R.wu_s)]
+    for copy in get_down:
+        copy.wait_recv()
+    relay_d = [copies.start(R.wd_s.at[down_rows(1, 0, 2), :], R.wd_s.at[down_rows(3, 0, 2), :], near[2]),
+               copies.start(R.wd_s.at[down_rows(2, 1, 2), :], R.wd_s.at[down_rows(3, 1, 2), :], near[1])]
+    mix(1)
+    get_i[0].relay()
+    for copy in relay_d:
+        copy.wait_recv()
     shared += [pass_on(R.wd_s.at[down_rows(j), :], sibling) for j in (1, 2, 3)]
     twin_a = [copies.start(R.act.at[:, other], R.twin_act, sibling),
               copies.start(R.o, R.twin_o, sibling)]
     load_dy.wait()
     for copy in load_f:
         copy.wait()
-    for copy in get_dy + shared + get_i:
-        copy.wait_recv()
+    get_i[1].relay()
+    for copy in get_dy + shared:
+        copy.wait_recv()
+    for part in get_i:
+        part.wait()
+    twin = [copies.start(R.inner.at[:, other], R.twin_inner, sibling),
+            copies.start(R.dyall.at[:, other], R.twin_dy, sibling)]
 
     def hidden_tile(t, carry):
         cs = aligned(t * ff, ff, 128)
@@ -628,50 +710,54 @@
 
     lax.fori_loop(0, hid_n, hidden_tile, 0)
 
-    twin = [copies.start(ref.at[pl.ds(0, n), :], ref.at[pl.ds(n, n), :], sibling)
+    twin += [copies.start(ref.at[pl.ds(0, n), :], ref.at[pl.ds(n, n), :], sibling)
             for ref in (R.hidden, R.ggate, R.gup)]
-    twin += [copies.start(R.inner.at[:, other], R.twin_inner, sibling),
-             copies.start(R.dyall.at[:, other], R.twin_dy, sibling)]
 
     def grad_tile(t, carry):
         cs = aligned(t * col, col, 128)
-        R.gin[:, cs] = (dot(R.ggate[0:n, :], R.wg_s[cs, :], 1, 1)
-                        + dot(R.gup[0:n, :], R.wu_s[cs, :], 1, 1)).astype(BF)
+        tile = (dot(R.ggate[0:n, :], R.wg_s[cs, :], 1, 1) + dot(R.gup[0:n, :], R.wu_s[cs, :], 1, 1)).astype(BF)
+        for w in range(wid_n):
+            for hh in range(2):
+                R.gin[w * sub + hh * step_n:w * sub + (hh + 1) * step_n, cs] = (
+                    tile[hh * part_n + w * step_n:hh * part_n + (w + 1) * step_n, :])
         return carry
 
     lax.fori_loop(0, wid_n, grad_tile, 0)
-    get_g = []
-    for slot, i in enumerate(order):
-        peer = place.wid_peer(i)
-        rows = aligned(peer * sub, sub, sub)
-        get_g.append(copies.start(R.gin.at[rows, :], R.recv_s.at[slot], {"wid": peer}))
-
-    copies.sent(shared + relay + [get_gate3] + get_a)
+    before = list(copies.open)
+    get_g = LineSwap(copies, place, lambda c: R.gin.at[aligned(c * sub, sub, sub), :],
+                     lambda q: R.recv_s.at[q] if q < 3 else R.recv_far)
+    get_g.start_far()
+    get_g.start()
+
+    copies.sent(before)
+    get_g.combine()
     for copy in twin:
         copy.wait_recv()
     R.left_t[:, 0:n] = R.inner[:, mine].T
     R.left_t[:, n:2 * n] = R.twin_inner[...].T
     down_a, down_b = pl.ds(0, half // 2), pl.ds(half // 2, half // 2)
 
-    def grads_tile(j, carry):
-        cs = aligned(j * ff, ff, 128)
+    upper, lower = pl.ds(0, half), pl.ds(half, half)
+
+    def ffn_grads(j):
+        cs = slice(j * ff, (j + 1) * ff)
         R.wg_s[0:half, cs] = dot(R.left_t[...], R.ggate[:, cs], 1, 0).astype(BF)
         R.wg_s[half:2 * half, cs] = dot(R.left_t[...], R.gup[:, cs], 1, 0).astype(BF)
         down = dot(R.hidden[0:n, cs], R.dyall[:, mine], 0, 0) + dot(R.hidden[n:2 * n, cs], R.twin_dy[...], 0, 0)
-        R.wu_s[aligned(j * ff, ff, ff), 0:half] = down.astype(BF)
-        return carry
-
-    lax.fori_loop(0, hid_n, grads_tile, 0)
-    upper, lower = pl.ds(0, half), pl.ds(half, half)
+        R.wu_s[cs, 0:half] = down.astype(BF)
 
     def first_round(j, slot, rows, lanes, to, gus, downs):
         return [copies.start(R.wg_s.at[rows, cols_of(j)], gus.at[slot], to),
                 copies.start(R.wu_s.at[cols_of(j), lanes], downs.at[slot], to)]
 
+    ffn_grads(3)
     get_r1 = (first_round(3, 1, upper, down_a, near[1], R.gu_x, R.dn_x)
-              + first_round(3, 1, lower, down_b, near[2], R.gu_y, R.dn_y)
-              + first_round(1, 0, upper, down_a, near[1], R.gu_x, R.dn_x)
-              + first_round(2, 0, lower, down_b, near[2], R.gu_y, R.dn_y))
+              + first_round(3, 1, lower, down_b, near[2], R.gu_y, R.dn_y))
+    ffn_grads(1)
+    keep_r1 = first_round(1, 0, upper, down_a, near[1], R.gu_x, R.dn_x)
+    ffn_grads(2)
+    keep_r1 += first_round(2, 0, lower, down_b, near[2], R.gu_y, R.dn_y)
+    ffn_grads(0)
 
     def out_tile(t, carry):
         cs = aligned(t * col, col, 128)
@@ -680,20 +766,25 @@
 
     lax.fori_loop(0, wid_n, out_tile, 0)
 
-    g_inner = R.gin[my_rows, :].astype(F32)
-    for slot, copy in enumerate(get_g):
-        copy.wait_recv()
-        g_inner = g_inner + R.recv_s[slot].astype(F32)
+    g_inner = get_g.total(R.gin[aligned(place.wid * sub, sub, sub), :].astype(F32))
     mixed = R.mixed[...]
     inv_two = lax.rsqrt(jnp.mean(mixed * mixed, -1, keepdims=True) + eps_norm)
     n_two = mixed * inv_two
     scaled = g_inner * R.gall[1:2, :]
-    g_mixed = (R.dyall[my_rows, :].astype(F32)
+    g_mixed = (own_rows(R.dyall)
                + inv_two * (scaled - n_two * jnp.mean(scaled * n_two, -1, keepdims=True)))
     R.row_g[...] = g_mixed.astype(BF)
-    get_z = [copies.start(R.row_g, R.gz.at[my_rows, :], d) for d in to_wid]
-    R.gz[my_rows, :] = R.row_g[...]
+    get_z = []
+    for hh in range(2):
+        at = rows_of(place.wid, hh)
+        get_z.append(LineGather(copies, place, R.row_g.at[pl.ds(hh * step_n, step_n), :],
+                                functools.partial(lambda hh, c: R.gz.at[rows_of(c, hh), :], hh)))
+        R.gz[at, :] = R.row_g[half_of(hh), :]
     R.gpart[1:2, :] = jnp.sum(g_inner * n_two, 0, keepdims=True)
+    for copy in twin_a:
+        copy.wait_recv()
+    for part in get_z:
+        part.relay()
     get_f = []
     for slot, i in enumerate(order):
         peer = place.wid_peer(i)
@@ -712,17 +803,15 @@
     get_r2 = [copies.start(add_g, R.gu_x.at[2], near[2]), copies.start(add_a, R.dn_x.at[2], near[2]),
               copies.start(add_u, R.gu_y.at[2], near[1]), copies.start(add_b, R.dn_y.at[2], near[1])]
 
-    for copy in twin_a:
-        copy.wait_recv()
-    for copy in get_z:
-        copy.wait_recv()
+    for part in get_z:
+        part.wait()
     twin_z = copies.start(R.gz.at[:, other], R.twin_gz, sibling)
 
     gets = [[] for _ in range(heads)]
     for h in range(heads):
         cs = head_cols(h)
         go = dot(R.gz[...], R.wo_s[cs, :], 1, 1).astype(BF)
-        attn_bwd_head(hops, h, R.probs, go, R.qt, R.v, R.fv, R.fp, R.chain,
+        attn_bwd_head(hops, h, R.probs, R.rcp, go, R.qt, R.v, R.fv, R.fp, R.chain,
                       R.gqt, R.near_s, R.gv, R.sendk, R.sendv, R.sendp, R.s_s)
         for i in range(1, hops + 1):
             to = place.row_peer(-i)
@@ -738,32 +827,39 @@
     twin_z.wait_recv()
     left_of(R.gz, R.twin_gz)
 
+    fine = piece // 2
     get_h = []
 
-    def spread(src, dst):
-        for j in range(1, hid_n):
-            p = turned(place.hid, j)
-            get_h.append(copies.start(src.at[aligned(p * piece, piece, 64), :], dst.at[j - 1], near[j]))
+    def rows_at(j, lot):
+        return aligned(turned(place.hid, j) * piece + lot * fine, fine, 32)
+
+    def round_one(src, slot):
+        sent = [copies.start(src.at[rows_at(3, lot), :], R.recv_q.at[slot, 2 * lot + 1], near[lot + 1]) for lot in range(2)]
+        keep = [copies.start(src.at[rows_at(lot + 1, lot), :], R.recv_q.at[slot, 2 * lot], near[lot + 1]) for lot in range(2)]
+        get_h.extend(keep)
+        return sent
+
+    def round_two(src, slot, sent):
+        for lot in range(2):
+            sent[lot].wait_recv()
+            at = src.at[rows_at(2 - lot, lot), :]
+            at[...] = (at[...].astype(F32) + R.recv_q[slot, 2 * lot + 1].astype(F32)).astype(BF)
+            get_h.append(copies.start(at, R.recv_q.at[slot, 4 + lot], near[2 - lot]))
 
     R.wide_s[...] = dot(R.left_t[:, 0:n], R.o[...], 1, 0) + dot(R.left_t[:, n:2 * n], R.twin_o[...], 1, 0)
     R.d_out[...] = R.wide_s[aligned(place.hid * piece, piece, 64), :]
     R.send_o[...] = R.wide_s[...].astype(BF)
-    spread(R.send_o, R.recv_o)
+    slot_o, slot_v = heads + 1, heads
+    sent_o = round_one(R.send_o, slot_o)
     left_of(R.act, R.twin_act)
 
     row8 = lax.broadcasted_iota(jnp.int32, (n, HDIM), 1)
     gc_all = jnp.zeros((n, HDIM), F32)
-    for h in range(heads):
-        for copy in gets[h]:
-            copy.wait_recv()
-        cs = head_cols(h)
-        gv = R.gv[:, cs]
-        for i in range(hops):
-            gv = gv + R.recvv[i, :, cs].astype(F32)
-        R.grads[0:n, (9 + h) * HDIM:(10 + h) * HDIM] = gv.astype(BF)
     val_cols = pl.ds(3 * width, width)
-    twin_v = copies.start(R.grads.at[pl.ds(0, n), val_cols], R.grads.at[pl.ds(n, n), val_cols], sibling)
     twin_h = []
+
+    def grad_part(slot):
+        return R.wd_s.at[:, pl.ds(slot * width, width)]
 
     def weights_of(slot, outs_of):
         cs = slice(slot * width, (slot + 1) * width)
@@ -772,20 +868,28 @@
         own = R.wide_s[aligned(place.hid * piece, piece, 64), :]
         for m, (ref, at) in enumerate(outs_of):
             ref[:, at] = own[:, head_cols(m)]
-        spread(R.wd_s.at[:, pl.ds(slot * width, width)], R.recv_q.at[:, :, pl.ds(slot * width, width)])
+        return round_one(grad_part(slot), slot)
 
     def outs_of(h):
         return [(ref, head_cols(h)) for ref in (R.d_query, R.d_key, R.d_house)]
 
     val_outs = [(R.d_value, head_cols(m)) for m in range(heads)]
+    sent_h = []
     for h in range(heads):
+        for copy in gets[h]:
+            copy.wait_recv()
         cs = head_cols(h)
         gkt = R.recvk[0, :, cs].astype(F32)
+        gv = R.gv[:, cs] + R.recvv[0, :, cs].astype(F32)
         for i in range(1, hops):
             gkt = gkt + R.recvk[i, :, cs].astype(F32)
+            gv = gv + R.recvv[i, :, cs].astype(F32)
         gp = R.recvp[0, h].astype(F32)
         for i in range(1, hops - 1):
             gp = gp + R.recvp[i, h].astype(F32)
+        R.grads[0:n, (9 + h) * HDIM:(10 + h) * HDIM] = gv.astype(BF)
+        if h == heads - 1:
+            twin_v = copies.start(R.grads.at[pl.ds(0, n), val_cols], R.grads.at[pl.ds(n, n), val_cols], sibling)
         gq, gk, gr, gc = path_bwd_head(h, heads, Heads(R.proj, 0), Heads(R.proj, 1), Heads(R.proj, 2), R.c,
                                        R.u, R.inv, R.psi, R.x1, R.y1, R.gqt[:, cs], gkt, R.near_s[h], gp)
         gc_all = jnp.where(row8 == h, gc, gc_all)
@@ -793,35 +897,42 @@
             R.grads[0:n, (3 * h + m) * HDIM:(3 * h + m + 1) * HDIM] = val
         gs = pl.ds(h * width, width)
         twin_h.append(copies.start(R.grads.at[pl.ds(0, n), gs], R.grads.at[pl.ds(n, n), gs], sibling))
-        if h == 0:
-            twin_v.wait_recv()
-            weights_of(heads, val_outs)
-        else:
+        if 0 < h:
             twin_h[h - 1].wait_recv()
-            weights_of(h - 1, outs_of(h - 1))
+            sent_h.append(weights_of(h - 1, outs_of(h - 1)))
     R.gcs[0:n, :] = gc_all.astype(BF)
     twin_c = copies.start(R.gcs.at[pl.ds(0, n), :], R.gcs.at[pl.ds(n, n), :], sibling)
 
     inv_rms = R.inv_rms[...]
     stat = jnp.zeros((n, 1), F32)
-    get_n = []
-    for slot, i in enumerate(order + [0]):
-        peer = place.wid_peer(i)
-        cs = aligned(peer * col, col, 128)
+    get_n = LineSwap(copies, place, lambda c: R.send_n.at[c], lambda q: R.recv_n.at[q])
+    me, side = place.wid, place.wid // 2
+    for turn, c in enumerate((3 * (1 - side), 2 - side, (1 - side) * (1 - me) + side * (5 - me), me)):
+        cs = aligned(c * col, col, 128)
         g_act = dot(R.grads[0:n, :], R.w_s[cs, :], 1, 1) + dot(R.gcs[0:n, 0:heads], R.wb[:, cs], 1, 0)
         normed = R.xall[:, cs].astype(F32) * inv_rms
         both = g_act * normed
         stat = stat + jnp.sum(both * R.gall[0:1, cs], 1, keepdims=True)
         R.gpart[0:1, cs] = jnp.sum(both, 0, keepdims=True)
-        if i == 0:
+        if turn == 3:
             R.own_n[...] = g_act
         else:
-            R.send_n[slot] = g_act.astype(BF)
-            get_n.append(copies.start(R.send_n.at[slot], R.recv_n.at[slot], {"wid": peer}))
+            R.send_n[c] = g_act.astype(BF)
+        if turn == 0:
+            get_n.start_far()
+        if turn == 2:
+            get_n.start()
     R.stat_s[...] = jnp.broadcast_to(stat, (n, HDIM)).T[0:8, :]
     get_s = [copies.start(R.stat_s, R.recv_st.at[slot], d) for slot, d in enumerate(to_wid)]
+    twin_v.wait_recv()
+    sent_v = weights_of(slot_v, val_outs)
+    get_n.combine()
     twin_h[heads - 1].wait_recv()
-    weights_of(heads - 1, outs_of(heads - 1))
+    sent_h.append(weights_of(heads - 1, outs_of(heads - 1)))
+    round_two(R.send_o, slot_o, sent_o)
+    for h in range(heads - 1):
+        round_two(grad_part(h), h, sent_h[h])
+    round_two(grad_part(slot_v), slot_v, sent_v)
     twin_c.wait_recv()
     d_beta = dot(R.gcs[0:n, :], R.act[:, mine], 0, 0) + dot(R.gcs[n:2 * n, :], R.twin_act[...], 0, 0)
     R.beta_s[...] = d_beta[0:8, :]
@@ -834,13 +945,14 @@
     get_gain = [copies.start(R.gpart.at[:, window(lax.rem(place.row + i, place.rows_n))], R.recv_gain.at[i - 1],
                              place.row_peer(i)) for i in range(1, place.rows_n)]
 
+    round_two(grad_part(heads - 1), heads - 1, sent_h[heads - 1])
     gain = R.gpart[:, window(place.row)]
     for i, copy in enumerate(get_gain):
         copy.wait_recv()
         gain = gain + R.recv_gain[i]
     R.gain_s[...] = gain
     get_gain2 = [copies.start(R.gain_s, R.recv_gain2.at[slot], d) for slot, d in enumerate(to_wid)]
-    for copy in get_r2:
+    for copy in get_r2 + keep_r1:
         copy.wait_recv()
     R.d_gate[...] = (R.wg_s[upper, 0:ff].astype(F32) + R.gu_x[0].astype(F32) + R.gu_x[2].astype(F32))
     R.d_up[...] = (R.wg_s[lower, 0:ff].astype(F32) + R.gu_y[0].astype(F32) + R.gu_y[2].astype(F32))
@@ -851,12 +963,10 @@
         copy.wait_recv()
         out = out + R.recv_f[slot].astype(F32)
     R.output[...] = out.astype(BF)
-    g_act = R.own_n[...]
+    g_act = get_n.total(R.own_n[...])
     stats = R.stat_s[...]
     for slot in range(wid_n - 1):
         get_s[slot].wait_recv()
-        get_n[slot].wait_recv()
-        g_act = g_act + R.recv_n[slot].astype(F32)
         stats = stats + R.recv_st[slot]
     mean = stats.T[:, 0:1] / model
     normed = R.xall[:, my_cols].astype(F32) * inv_rms
@@ -864,15 +974,13 @@
                        + inv_rms * (g_act * R.gall[0:1, my_cols] - normed * mean))
     for copy in get_h + get_b:
         copy.wait_recv()
-    for i in range(hid_n - 1):
-        R.d_out[...] += R.recv_o[i].astype(F32)
-    for slot, refs_of in [(heads, val_outs)] + [(h, outs_of(h)) for h in range(heads)]:
+    out_outs = [(R.d_out, head_cols(m)) for m in range(heads)]
+    for slot, refs_of in [(slot_o, out_outs), (slot_v, val_outs)] + [(h, outs_of(h)) for h in range(heads)]:
         for m, (ref, at) in enumerate(refs_of):
-            base = slot * width + m * HDIM
-            total = ref[:, at]
-            for i in range(hid_n - 1):
-                total = total + R.recv_q[i, :, base:base + HDIM].astype(F32)
-            ref[:, at] = total
+            for lot in range(2):
+                rs = slice(lot * fine, (lot + 1) * fine)
+                ref[rs, at] = (ref[rs, at] + R.recv_q[slot, 2 * lot, :, head_cols(m)].astype(F32)
+                               + R.recv_q[slot, 4 + lot, :, head_cols(m)].astype(F32))
     d_beta = R.beta_s[:, window(place.hid)]
     for i in range(hid_n - 1):
         d_beta = d_beta + R.recv_b[i]
@@ -917,13 +1025,13 @@
         qt=V((n, width), BF), u=V((n, width), F32), inv=V((heads, n, n), F32), psi=V((heads, n, n), F32),
         x1=V((n, width), F32), y1=V((n, width), F32),
         fv=V((hops, n, width), BF), fp=V((hops - 1, heads, HDIM, HDIM), BF), chain=V((slots, n, width), BF),
-        probs=V((hops + 1, heads, n, n), BF), o=V((n, width), BF), mixed=V((sub, model), F32),
+        probs=V((hops + 1, heads, n, n), BF), rcp=V((n, heads), F32), o=V((n, width), BF), mixed=V((sub, model), F32),
         inner=V((n, model), BF), hidden=V((2 * n, hid_n * ff), BF), ggate=V((2 * n, hid_n * ff), BF),
         gup=V((2 * n, hid_n * ff), BF), gin=V((n, model), BF),
         w_s=V((model, 4 * width), BF), wo_s=V((width, model), BF),
         wg_s=V((model, hid_n * ff), BF), wu_s=V((model, hid_n * ff), BF), wd_s=V((hid_n * ff, model), BF),
         kt_s=V((n, width), BF), near_s=V((heads, n, n), F32), prod_s=V((heads, HDIM, HDIM), BF),
-        s_s=V(((hops + 1) * n, n), F32), part_s=V((n, model), BF), recv_s=V((peers_w, sub, model), BF),
+        s_s=V(((hops + 1) * n, n), F32), part_s=V((n, model), BF), recv_s=V((wid_n, sub, model), BF), recv_far=V((sub, model), BF),
         row_s=V((sub, model), BF), row_g=V((sub, model), BF),
         twin_inner=V((n, half), BF), twin_dy=V((n, half), BF), twin_act=V((n, half), BF), twin_o=V((n, width), BF),
         twin_gz=V((n, half), BF), left_t=V((half, 2 * n), BF),
@@ -933,14 +1041,14 @@
         gqt=V((n, width), F32), gv=V((n, width), F32),
         sendk=V((hops, n, width), BF), sendv=V((hops, n, width), BF), sendp=V((hops - 1, heads, HDIM, HDIM), BF),
         recvk=V((hops, n, width), BF), recvv=V((hops, n, width), BF), recvp=V((hops - 1, heads, HDIM, HDIM), BF),
-        send_o=V((half, width), BF), recv_o=V((peers_h, piece, width), BF),
+        send_o=V((half, width), BF),
         grads=V((2 * n, 4 * width), BF), gcs=V((2 * n, HDIM), BF), wide_s=V((half, width), F32),
-        recv_q=V((peers_h, piece, 4 * width), BF), beta_s=V((8, half), F32), recv_b=V((peers_h, 8, 256), F32),
-        own_n=V((n, col), F32), send_n=V((peers_w, n, col), BF), recv_n=V((peers_w, n, col), BF),
+        recv_q=V((heads + 2, 6, piece // 2, width), BF), beta_s=V((8, half), F32), recv_b=V((peers_h, 8, 256), F32),
+        own_n=V((n, col), F32), send_n=V((wid_n, n, col), BF), recv_n=V((wid_n, n, col), BF),
         stat_s=V((8, n), F32), recv_st=V((peers_w, 8, n), F32),
         recv_gain=V((rows_n - 1, 8, 256), F32), gain_s=V((8, 256), F32), recv_gain2=V((peers_w, 8, 256), F32),
     )
-    n_copies = 200
+    n_copies = 256
     scratch.update(load_sem=pltpu.SemaphoreType.DMA((24,)), send_sem=pltpu.SemaphoreType.DMA((n_copies,)),
                    recv_sem=pltpu.SemaphoreType.DMA((n_copies,)))
     spaces = {"lengths": pltpu.SMEM, "x": pltpu.VMEM, "gain_attn": pltpu.VMEM, "gain_ffn": pltpu.VMEM, "wb": pltpu.VMEM}
@@ -1041,7 +1149,7 @@
     far_k = jnp.stack([shifted(kt, ROWS, i) for i in range(1, hops + 1)])
     far_p = jnp.stack([shifted(prod, ROWS, i) for i in range(1, hops)])
     row_arr = jnp.full((1,), my_row, jnp.int32)
-    attended, probs, chain = attn_fwd(lengths, row_arr, qt, near, v, far_k, far_v, far_p, heads, hops)
+    attended, probs, chain, rcp = attn_fwd(lengths, row_arr, qt, near, v, far_k, far_v, far_p, heads, hops)
 
     attn_part = jnp.dot(attended, w_out, preferred_element_type=F32).astype(BF)
     attn_rows = lax.psum_scatter(attn_part, "wid", scatter_dimension=0, tiled=True)
@@ -1078,7 +1186,7 @@
 
     g_attn = jnp.einsum("tc,ic->ti", g_z, w_out, preferred_element_type=F32).astype(BF)
     d_out = jnp.einsum("ti,tc->ic", attended, g_z, preferred_element_type=F32).astype(BF)
-    g_qt, g_near, gv, send_k, send_v, send_p = attn_bwd(probs, g_attn, qt, v, far_v, far_p, chain, heads, hops)
+    g_qt, g_near, gv, send_k, send_v, send_p = attn_bwd(probs, rcp, g_attn, qt, v, far_v, far_p, chain, heads, hops)
     g_kt = sum(shifted(send_k[i - 1], ROWS, -i).astype(F32) for i in range(1, hops + 1))
     gv = gv + sum(shifted(send_v[i - 1], ROWS, -i).astype(F32) for i in range(1, hops + 1))
     g_prod = sum(shifted(send_p[i - 1], ROWS, -i).astype(F32) for i in range(1, hops))
@@ -1139,7 +1247,7 @@
 
 
 def slow(mesh):
-    return (mesh.shape["seq"], mesh.shape["hid"]) != (2, 4)
+    return (mesh.shape["seq"], mesh.shape["hid"], mesh.shape["wid"]) != (2, 4, 4)
 
 
 def solution(mesh):

time: 216 us -> 191 us (0.88)
  Pallas kernels: 214 us -> 189 us
    pallas_call x1, Pallas kernels: 210 us -> 185 us  [step(): pl.pallas_call(functools.partial(step_kernel, (heads, hops, sizes), ins +...]
where the time goes in v1:
time: 191 us
  Pallas kernels  189 us (99%)
    pallas_call x1, Pallas kernels, step(): pl.pallas_call(functools.partial(step_kernel, (heads, hops, sizes), ins +...  185 us
    pallas_call x1, Pallas kernels, finish(): pl.pallas_call(functools.partial(finish_kernel, count), in_specs=[spec] *...  4.24 us

profile of v1, /device:TPU:0, one launch (start us, length us, event | category | flops | bytes accessed | tf_op | source)
XLA Modules:
  0.0 191.2 jit_solution(14555344725807754123)
XLA Ops:
  0.7 185.0 %step.1 = (bf16[256,384]{1,0:T(8,128)(2,1)}, f32[256,384]{1,0:T(8,128)}, f32[8,192]{1,0:T(8,128)}, f32[192,384]{1,0:T(8,128)}, f32[192,384]{1,0:T(8,128)}, /*ind...) custom-call(s32[3]{0:T(128)} %refs_0_.1, ...), custom_call_target="tpu_custom_call" | custom-call | tf_op jit(solution)/shard_map/step/pallas_call | solution.py:1056
  185.6 4.2 %finish.1 = (bf16[256,384]{1,0:T(8,128)(2,1)}, f32[256,384]{1,0:T(8,128)}, f32[192,384]{1,0:T(8,128)}, f32[192,384]{1,0:T(8,128)}, f32[192,384]{1,0:T(8,128)}, /...) custom-call(bf16[256,384]{1,0:T(8,128)(2,1)} %get-tuple-element.36.r, ...), custom_call_target="tpu_custom_call" | custom-call | tf_op jit(solution)/shard_map/finish/pallas_call | solution.py:1085
  189.9 1.3 fusion

commit v2 on v1

--- a/solution.py
+++ b/solution.py
@@ -81,29 +81,29 @@
         return carry
 
     lax.fori_loop(1, (n - 1).bit_length(), double, 0)
+    er, ec = iotas(HDIM)
+    for h in range(heads):
+        kin = split(inv_ref[h])
+        k = k_ref[:, head_cols(h)]
+        u2 = us2[h]
+        aq = jnp.where(rows < cols, dot3(split(k), u2, 1, 1), 0.0)
+        y = dot3(kin, u2, 0, 0)
+        y_ref[:, head_cols(h)] = y
+        kt_ref[:, head_cols(h)] = (k - dot3(split(aq), split(y), 1, 0)).astype(BF)
+        x = dot3(kin, u2, 1, 0)
+        x_ref[:, head_cols(h)] = x
+        p_ref[h] = (jnp.where(er == ec, 1.0, 0.0) - dot3(u2, split(x), 0, 0)).astype(p_ref.dtype)
+        if done is not None:
+            done(h)
     for h in range(heads):
         kin = split(inv_ref[h])
         q = q_ref[:, head_cols(h)]
-        k = k_ref[:, head_cols(h)]
-        q2, k2, u2 = split(q), split(k), us2[h]
-        a = jnp.where(rows > cols, dot3(u2, k2, 1, 1), 0.0)
-        aq = jnp.where(rows < cols, dot3(k2, u2, 1, 1), 0.0)
-        fq = jnp.where(rows >= cols, dot3(q2, u2, 1, 1), 0.0)
-        fq2 = split(fq)
-        x = dot3(kin, u2, 1, 0)
-        y = dot3(kin, u2, 0, 0)
-        psi = dot3(kin, split(a), 1, 0)
-        x2 = split(x)
-        x_ref[:, head_cols(h)] = x
-        y_ref[:, head_cols(h)] = y
+        q2, k2, u2, x2 = split(q), split(k_ref[:, head_cols(h)]), us2[h], split(x_ref[:, head_cols(h)])
+        fq2 = split(jnp.where(rows >= cols, dot3(q2, u2, 1, 1), 0.0))
+        qt_ref[:, head_cols(h)] = (q - dot3(fq2, x2, 1, 0)).astype(BF)
+        psi = dot3(kin, split(jnp.where(rows > cols, dot3(u2, k2, 1, 1), 0.0)), 1, 0)
         psi_ref[h] = psi
-        qt_ref[:, head_cols(h)] = (q - dot3(fq2, x2, 1, 0)).astype(BF)
-        kt_ref[:, head_cols(h)] = (k - dot3(split(aq), split(y), 1, 0)).astype(BF)
         near_ref[h] = dot3(q2, k2, 1, 1) - dot3(fq2, split(psi), 1, 0)
-        er, ec = iotas(HDIM)
-        p_ref[h] = (jnp.where(er == ec, 1.0, 0.0) - dot3(u2, x2, 0, 0)).astype(p_ref.dtype)
-        if done is not None:
-            done(h)
 
 
 def path_fwd_kernel(heads, *refs):
@@ -696,8 +696,15 @@
     twin = [copies.start(R.inner.at[:, other], R.twin_inner, sibling),
             copies.start(R.dyall.at[:, other], R.twin_dy, sibling)]
 
+    swapped = (R.hidden, R.ggate, R.gup)
+    swap_ids = [copies.take() for _ in range(3 * hid_n)]
+
+    def swap(m, cs, i):
+        return copies.make(swapped[m].at[pl.ds(0, n), cs], swapped[m].at[pl.ds(n, n), cs], sibling, i, i)
+
     def hidden_tile(t, carry):
-        cs = aligned(t * ff, ff, 128)
+        j = hid_n - 1 - t
+        cs = aligned(j * ff, ff, 128)
         gate = dot(R.inner[...], R.wg_s[:, cs], 1, 0)
         up = dot(R.inner[...], R.wu_s[:, cs], 1, 0)
         g_hidden = dot(R.dyall[...], R.wd_s[cs, :], 1, 1)
@@ -706,12 +713,39 @@
         R.hidden[0:n, cs] = (silu * up).astype(BF)
         R.ggate[0:n, cs] = (g_hidden * up * sig * (1.0 + gate * (1.0 - sig))).astype(BF)
         R.gup[0:n, cs] = (g_hidden * silu).astype(BF)
+        for m in range(3):
+            swap(m, cs, swap_ids[0] + 3 * j + m).start()
         return carry
 
     lax.fori_loop(0, hid_n, hidden_tile, 0)
-
-    twin += [copies.start(ref.at[pl.ds(0, n), :], ref.at[pl.ds(n, n), :], sibling)
-            for ref in (R.hidden, R.ggate, R.gup)]
+    twin_tile = [[swap(m, cols_of(j), swap_ids[3 * j + m]) for m in range(3)] for j in range(hid_n)]
+    for tile in twin_tile:
+        copies.open.extend(tile)
+    before = list(copies.open)
+
+    for copy in twin:
+        copy.wait_recv()
+    R.left_t[:, 0:n] = R.inner[:, mine].T
+    R.left_t[:, n:2 * n] = R.twin_inner[...].T
+    down_a, down_b = pl.ds(0, half // 2), pl.ds(half // 2, half // 2)
+    upper, lower = pl.ds(0, half), pl.ds(half, half)
+
+    def ffn_grads(j, gate_up, down):
+        for copy in twin_tile[j]:
+            copy.wait_recv()
+        cs = slice(j * ff, (j + 1) * ff)
+        gate_up[0:half, :] = dot(R.left_t[...], R.ggate[:, cs], 1, 0).astype(BF)
+        gate_up[half:2 * half, :] = dot(R.left_t[...], R.gup[:, cs], 1, 0).astype(BF)
+        down[...] = (dot(R.hidden[0:n, cs], R.dyall[:, mine], 0, 0)
+                     + dot(R.hidden[n:2 * n, cs], R.twin_dy[...], 0, 0)).astype(BF)
+
+    def first_round(gate_up, down, slot, rows, lanes, to, gus, downs):
+        return [copies.start(gate_up.at[rows, :], gus.at[slot], to),
+                copies.start(down.at[:, lanes], downs.at[slot], to)]
+
+    ffn_grads(3, R.far_gu, R.far_dn)
+    get_r1 = (first_round(R.far_gu, R.far_dn, 1, upper, down_a, near[1], R.gu_x, R.dn_x)
+              + first_round(R.far_gu, R.far_dn, 1, lower, down_b, near[2], R.gu_y, R.dn_y))
 
     def grad_tile(t, carry):
         cs = aligned(t * col, col, 128)
@@ -723,41 +757,21 @@
         return carry
 
     lax.fori_loop(0, wid_n, grad_tile, 0)
-    before = list(copies.open)
     get_g = LineSwap(copies, place, lambda c: R.gin.at[aligned(c * sub, sub, sub), :],
                      lambda q: R.recv_s.at[q] if q < 3 else R.recv_far)
     get_g.start_far()
     get_g.start()
-
     copies.sent(before)
+
+    def grads_of(j):
+        return R.wg_s.at[:, cols_of(j)], R.wu_s.at[cols_of(j), pl.ds(0, half)]
+
+    ffn_grads(2, *grads_of(2))
+    keep_r1 = first_round(*grads_of(2), 0, lower, down_b, near[2], R.gu_y, R.dn_y)
+    ffn_grads(1, *grads_of(1))
+    keep_r1 += first_round(*grads_of(1), 0, upper, down_a, near[1], R.gu_x, R.dn_x)
     get_g.combine()
-    for copy in twin:
-        copy.wait_recv()
-    R.left_t[:, 0:n] = R.inner[:, mine].T
-    R.left_t[:, n:2 * n] = R.twin_inner[...].T
-    down_a, down_b = pl.ds(0, half // 2), pl.ds(half // 2, half // 2)
-
-    upper, lower = pl.ds(0, half), pl.ds(half, half)
-
-    def ffn_grads(j):
-        cs = slice(j * ff, (j + 1) * ff)
-        R.wg_s[0:half, cs] = dot(R.left_t[...], R.ggate[:, cs], 1, 0).astype(BF)
-        R.wg_s[half:2 * half, cs] = dot(R.left_t[...], R.gup[:, cs], 1, 0).astype(BF)
-        down = dot(R.hidden[0:n, cs], R.dyall[:, mine], 0, 0) + dot(R.hidden[n:2 * n, cs], R.twin_dy[...], 0, 0)
-        R.wu_s[cs, 0:half] = down.astype(BF)
-
-    def first_round(j, slot, rows, lanes, to, gus, downs):
-        return [copies.start(R.wg_s.at[rows, cols_of(j)], gus.at[slot], to),
-                copies.start(R.wu_s.at[cols_of(j), lanes], downs.at[slot], to)]
-
-    ffn_grads(3)
-    get_r1 = (first_round(3, 1, upper, down_a, near[1], R.gu_x, R.dn_x)
-              + first_round(3, 1, lower, down_b, near[2], R.gu_y, R.dn_y))
-    ffn_grads(1)
-    keep_r1 = first_round(1, 0, upper, down_a, near[1], R.gu_x, R.dn_x)
-    ffn_grads(2)
-    keep_r1 += first_round(2, 0, lower, down_b, near[2], R.gu_y, R.dn_y)
-    ffn_grads(0)
+    ffn_grads(0, *grads_of(0))
 
     def out_tile(t, carry):
         cs = aligned(t * col, col, 128)
@@ -765,6 +779,19 @@
         return carry
 
     lax.fori_loop(0, wid_n, out_tile, 0)
+
+    for copy in get_r1:
+        copy.wait_recv()
+    add_g = R.wg_s.at[upper, cols_of(2)]
+    add_g[...] = (add_g[...].astype(F32) + R.gu_x[1].astype(F32)).astype(BF)
+    add_u = R.wg_s.at[lower, cols_of(1)]
+    add_u[...] = (add_u[...].astype(F32) + R.gu_y[1].astype(F32)).astype(BF)
+    add_a = R.wu_s.at[cols_of(2), down_a]
+    add_a[...] = (add_a[...].astype(F32) + R.dn_x[1].astype(F32)).astype(BF)
+    add_b = R.wu_s.at[cols_of(1), down_b]
+    add_b[...] = (add_b[...].astype(F32) + R.dn_y[1].astype(F32)).astype(BF)
+    get_r2 = [copies.start(add_g, R.gu_x.at[2], near[2]), copies.start(add_a, R.dn_x.at[2], near[2]),
+              copies.start(add_u, R.gu_y.at[2], near[1]), copies.start(add_b, R.dn_y.at[2], near[1])]
 
     g_inner = get_g.total(R.gin[aligned(place.wid * sub, sub, sub), :].astype(F32))
     mixed = R.mixed[...]
@@ -790,19 +817,6 @@
         peer = place.wid_peer(i)
         get_f.append(copies.start(R.part_s.at[:, aligned(peer * col, col, 128)], R.recv_f.at[slot], {"wid": peer}))
 
-    for copy in get_r1:
-        copy.wait_recv()
-    add_g = R.wg_s.at[upper, cols_of(2)]
-    add_g[...] = (add_g[...].astype(F32) + R.gu_x[1].astype(F32)).astype(BF)
-    add_u = R.wg_s.at[lower, cols_of(1)]
-    add_u[...] = (add_u[...].astype(F32) + R.gu_y[1].astype(F32)).astype(BF)
-    add_a = R.wu_s.at[cols_of(2), down_a]
-    add_a[...] = (add_a[...].astype(F32) + R.dn_x[1].astype(F32)).astype(BF)
-    add_b = R.wu_s.at[cols_of(1), down_b]
-    add_b[...] = (add_b[...].astype(F32) + R.dn_y[1].astype(F32)).astype(BF)
-    get_r2 = [copies.start(add_g, R.gu_x.at[2], near[2]), copies.start(add_a, R.dn_x.at[2], near[2]),
-              copies.start(add_u, R.gu_y.at[2], near[1]), copies.start(add_b, R.dn_y.at[2], near[1])]
-
     for part in get_z:
         part.wait()
     twin_z = copies.start(R.gz.at[:, other], R.twin_gz, sibling)
@@ -852,6 +866,13 @@
     slot_o, slot_v = heads + 1, heads
     sent_o = round_one(R.send_o, slot_o)
     left_of(R.act, R.twin_act)
+    for copy in get_r2 + keep_r1:
+        copy.wait_recv()
+    R.d_gate_s[...] = (R.wg_s[upper, 0:ff].astype(F32) + R.gu_x[0].astype(F32) + R.gu_x[2].astype(F32))
+    R.d_up_s[...] = (R.wg_s[lower, 0:ff].astype(F32) + R.gu_y[0].astype(F32) + R.gu_y[2].astype(F32))
+    for lanes, ref in ((down_a, R.dn_x), (down_b, R.dn_y)):
+        R.d_down_s[:, lanes] = R.wu_s[0:ff, lanes].astype(F32) + ref[0].astype(F32) + ref[2].astype(F32)
+    stores = [loads.start(R.d_gate_s, R.d_gate), loads.start(R.d_up_s, R.d_up), loads.start(R.d_down_s, R.d_down)]
 
     row8 = lax.broadcasted_iota(jnp.int32, (n, HDIM), 1)
     gc_all = jnp.zeros((n, HDIM), F32)
@@ -897,7 +918,7 @@
             R.grads[0:n, (3 * h + m) * HDIM:(3 * h + m + 1) * HDIM] = val
         gs = pl.ds(h * width, width)
         twin_h.append(copies.start(R.grads.at[pl.ds(0, n), gs], R.grads.at[pl.ds(n, n), gs], sibling))
-        if 0 < h:
+        if 0 < h < heads - 1:
             twin_h[h - 1].wait_recv()
             sent_h.append(weights_of(h - 1, outs_of(h - 1)))
     R.gcs[0:n, :] = gc_all.astype(BF)
@@ -924,45 +945,41 @@
             get_n.start()
     R.stat_s[...] = jnp.broadcast_to(stat, (n, HDIM)).T[0:8, :]
     get_s = [copies.start(R.stat_s, R.recv_st.at[slot], d) for slot, d in enumerate(to_wid)]
+
+    def window(p):
+        return aligned(p * piece // 128 * 128, 256, 128)
+
+    get_gain = [copies.start(R.gpart.at[:, window(lax.rem(place.row + i, place.rows_n))], R.recv_gain.at[i - 1],
+                             place.row_peer(i)) for i in range(1, place.rows_n)]
+    twin_c.wait_recv()
+    d_beta = dot(R.gcs[0:n, :], R.act[:, mine], 0, 0) + dot(R.gcs[n:2 * n, :], R.twin_act[...], 0, 0)
+    R.beta_s[...] = d_beta[0:8, :]
+    get_b = [copies.start(R.beta_s.at[:, window(turned(place.hid, j))], R.recv_b.at[j - 1], near[j])
+             for j in range(1, hid_n)]
+    for h in (heads - 2, heads - 1):
+        twin_h[h].wait_recv()
+        sent_h.append(weights_of(h, outs_of(h)))
+    get_n.combine()
     twin_v.wait_recv()
     sent_v = weights_of(slot_v, val_outs)
-    get_n.combine()
-    twin_h[heads - 1].wait_recv()
-    sent_h.append(weights_of(heads - 1, outs_of(heads - 1)))
     round_two(R.send_o, slot_o, sent_o)
     for h in range(heads - 1):
         round_two(grad_part(h), h, sent_h[h])
-    round_two(grad_part(slot_v), slot_v, sent_v)
-    twin_c.wait_recv()
-    d_beta = dot(R.gcs[0:n, :], R.act[:, mine], 0, 0) + dot(R.gcs[n:2 * n, :], R.twin_act[...], 0, 0)
-    R.beta_s[...] = d_beta[0:8, :]
-
-    def window(p):
-        return aligned(p * piece // 128 * 128, 256, 128)
-
-    get_b = [copies.start(R.beta_s.at[:, window(turned(place.hid, j))], R.recv_b.at[j - 1], near[j])
-             for j in range(1, hid_n)]
-    get_gain = [copies.start(R.gpart.at[:, window(lax.rem(place.row + i, place.rows_n))], R.recv_gain.at[i - 1],
-                             place.row_peer(i)) for i in range(1, place.rows_n)]
-
-    round_two(grad_part(heads - 1), heads - 1, sent_h[heads - 1])
+    out = R.x[...].astype(F32) + R.part_s[:, my_cols].astype(F32)
+    for slot, copy in enumerate(get_f):
+        copy.wait_recv()
+        out = out + R.recv_f[slot].astype(F32)
+    R.output_s[...] = out.astype(BF)
+    stores.append(loads.start(R.output_s, R.output))
     gain = R.gpart[:, window(place.row)]
     for i, copy in enumerate(get_gain):
         copy.wait_recv()
         gain = gain + R.recv_gain[i]
     R.gain_s[...] = gain
     get_gain2 = [copies.start(R.gain_s, R.recv_gain2.at[slot], d) for slot, d in enumerate(to_wid)]
-    for copy in get_r2 + keep_r1:
-        copy.wait_recv()
-    R.d_gate[...] = (R.wg_s[upper, 0:ff].astype(F32) + R.gu_x[0].astype(F32) + R.gu_x[2].astype(F32))
-    R.d_up[...] = (R.wg_s[lower, 0:ff].astype(F32) + R.gu_y[0].astype(F32) + R.gu_y[2].astype(F32))
-    for lanes, ref in ((down_a, R.dn_x), (down_b, R.dn_y)):
-        R.d_down[:, lanes] = R.wu_s[0:ff, lanes].astype(F32) + ref[0].astype(F32) + ref[2].astype(F32)
-    out = R.x[...].astype(F32) + R.part_s[:, my_cols].astype(F32)
-    for slot, copy in enumerate(get_f):
-        copy.wait_recv()
-        out = out + R.recv_f[slot].astype(F32)
-    R.output[...] = out.astype(BF)
+    round_two(grad_part(slot_v), slot_v, sent_v)
+
+    round_two(grad_part(heads - 1), heads - 1, sent_h[heads - 1])
     g_act = get_n.total(R.own_n[...])
     stats = R.stat_s[...]
     for slot in range(wid_n - 1):
@@ -994,6 +1011,8 @@
 
     R.d_beta[...] = exact(d_beta, place.hid)[0:heads, :]
     R.gain_out[...] = exact(gain, place.row)
+    for store in stores:
+        store.wait()
     copies.sent(copies.open)
 
 
@@ -1032,6 +1051,7 @@
         wg_s=V((model, hid_n * ff), BF), wu_s=V((model, hid_n * ff), BF), wd_s=V((hid_n * ff, model), BF),
         kt_s=V((n, width), BF), near_s=V((heads, n, n), F32), prod_s=V((heads, HDIM, HDIM), BF),
         s_s=V(((hops + 1) * n, n), F32), part_s=V((n, model), BF), recv_s=V((wid_n, sub, model), BF), recv_far=V((sub, model), BF),
+        far_gu=V((2 * half, ff), BF), far_dn=V((ff, half), BF),
         row_s=V((sub, model), BF), row_g=V((sub, model), BF),
         twin_inner=V((n, half), BF), twin_dy=V((n, half), BF), twin_act=V((n, half), BF), twin_o=V((n, width), BF),
         twin_gz=V((n, half), BF), left_t=V((half, 2 * n), BF),
@@ -1045,6 +1065,7 @@
         grads=V((2 * n, 4 * width), BF), gcs=V((2 * n, HDIM), BF), wide_s=V((half, width), F32),
         recv_q=V((heads + 2, 6, piece // 2, width), BF), beta_s=V((8, half), F32), recv_b=V((peers_h, 8, 256), F32),
         own_n=V((n, col), F32), send_n=V((wid_n, n, col), BF), recv_n=V((wid_n, n, col), BF),
+        output_s=V((n, col), BF), d_gate_s=V((half, ff), F32), d_up_s=V((half, ff), F32), d_down_s=V((ff, half), F32),
         stat_s=V((8, n), F32), recv_st=V((peers_w, 8, n), F32),
         recv_gain=V((rows_n - 1, 8, 256), F32), gain_s=V((8, 256), F32), recv_gain2=V((peers_w, 8, 256), F32),
     )
@@ -1053,11 +1074,12 @@
                    recv_sem=pltpu.SemaphoreType.DMA((n_copies,)))
     spaces = {"lengths": pltpu.SMEM, "x": pltpu.VMEM, "gain_attn": pltpu.VMEM, "gain_ffn": pltpu.VMEM, "wb": pltpu.VMEM}
     vmem = pl.BlockSpec(memory_space=pltpu.VMEM)
+    early = ("output", "d_gate", "d_up", "d_down")
     res = pl.pallas_call(
         functools.partial(step_kernel, (heads, hops, sizes), ins + tuple(outs) + tuple(scratch)),
         in_specs=[pl.BlockSpec(memory_space=spaces.get(i, pl.ANY)) for i in ins],
         out_shape=tuple(outs.values()),
-        out_specs=tuple(vmem for _ in outs),
+        out_specs=tuple(pl.BlockSpec(memory_space=pl.ANY) if i in early else vmem for i in outs),
         scratch_shapes=list(scratch.values()),
         compiler_params=pltpu.CompilerParams(
             vmem_limit_bytes=VMEM_ALL, collective_id=1, has_side_effects=True),
@@ -1067,29 +1089,45 @@
 
 
 def finish_kernel(count, *refs):
-    ins, outs, bufs, sems = refs[:count], refs[count:2 * count], refs[2 * count:3 * count], refs[3 * count]
-    loads = [pltpu.make_async_copy(a, b, sems.at[0, i]) for i, (a, b) in enumerate(zip(ins, bufs))]
-    stores = [pltpu.make_async_copy(b, c, sems.at[1, i]) for i, (b, c) in enumerate(zip(bufs, outs))]
+    ins, outs, bufs = refs[:count + 1], refs[count + 1:2 * count + 3], refs[2 * count + 3:3 * count + 4]
+    lines, sems = refs[3 * count + 4:3 * count + 6], refs[3 * count + 6]
+    loads, stores = [], []
+    for a, b, c in zip(ins[:count], bufs[:count], outs[:count]):
+        rows = a.shape[0]
+        cut = rows // 2 if rows >= 256 else rows
+        for start in range(0, rows, cut):
+            i, part = len(loads), pl.ds(start, cut)
+            loads.append(pltpu.make_async_copy(a.at[part, :], b.at[part, :], sems.at[0, i]))
+            stores.append(pltpu.make_async_copy(b.at[part, :], c.at[part, :], sems.at[1, i]))
+    last = len(loads)
+    loads.insert(0, pltpu.make_async_copy(ins[count], bufs[count], sems.at[0, last]))
     for copy in loads:
         copy.start()
-    for load, store in zip(loads, stores):
+    loads[0].wait()
+    for m in range(2):
+        lines[m][...] = bufs[count][m, :]
+        stores.append(pltpu.make_async_copy(lines[m], outs[count + m], sems.at[1, last + m]))
+        stores[-1].start()
+    for load, store in zip(loads[1:], stores):
         load.wait()
         store.start()
     for copy in stores:
         copy.wait()
 
 
-def finish(arrays):
-    count = len(arrays)
+def finish(arrays, gains):
+    count, size = len(arrays), gains.shape[1]
     spec = pl.BlockSpec(memory_space=pl.ANY)
+    vector = jax.ShapeDtypeStruct((size,), F32)
     return pl.pallas_call(
         functools.partial(finish_kernel, count),
-        in_specs=[spec] * count, out_specs=[spec] * count,
-        out_shape=[jax.ShapeDtypeStruct(a.shape, a.dtype) for a in arrays],
-        scratch_shapes=[pltpu.VMEM(a.shape, a.dtype) for a in arrays] + [pltpu.SemaphoreType.DMA((2, count))],
+        in_specs=[spec] * (count + 1), out_specs=[spec] * (count + 2),
+        out_shape=[jax.ShapeDtypeStruct(a.shape, a.dtype) for a in arrays] + [vector, vector],
+        scratch_shapes=([pltpu.VMEM(a.shape, a.dtype) for a in arrays + [gains]]
+                        + [pltpu.VMEM((size,), F32)] * 2 + [pltpu.SemaphoreType.DMA((2, 2 * count + 2))]),
         compiler_params=pltpu.CompilerParams(vmem_limit_bytes=VMEM_ALL),
         name="finish",
-    )(*arrays)
+    )(*arrays, gains)
 
 
 def shifted(array, axis, by):
@@ -1241,8 +1279,8 @@
     f = step((lengths, inputs, cotangent, gain_attn, gain_ffn, w_query, w_key, w_value, w_house,
               w_beta.T, w_out, w_gate, w_up, w_down), heads, hops, sizes)
     names = [i for i in f if i != "gain_out"]
-    f.update(zip(names, finish([f[i] for i in names])))
-    return (f["output"], f["d_inputs"], f["gain_out"][0], f["gain_out"][1], f["d_query"], f["d_key"], f["d_value"],
+    f.update(zip(names + ["gain_one", "gain_two"], finish([f[i] for i in names], f["gain_out"])))
+    return (f["output"], f["d_inputs"], f["gain_one"], f["gain_two"], f["d_query"], f["d_key"], f["d_value"],
             f["d_house"], f["d_beta"].T, f["d_out"].T, f["d_gate"], f["d_up"], f["d_down"])
 
 

time: 191 us -> 184 us (0.963); the launches traced: 191 us -> 182 us
  Pallas kernels: 189 us -> 181 us
    pallas_call x1, Pallas kernels: 185 us -> 176 us  [step(): pl.pallas_call(functools.partial(step_kernel, (heads, hops, sizes), ins +...]
where the time goes in v2:
time: 184 us; the launch traced here: 182 us
  Pallas kernels  181 us (98%)
    pallas_call x1, Pallas kernels, step(): pl.pallas_call(functools.partial(step_kernel, (heads, hops, sizes), ins +...  176 us
    pallas_call x1, Pallas kernels, finish(): pl.pallas_call(functools.partial(finish_kernel, count), in_specs=[spec] *...  4.7 us

profile of v2, /device:TPU:0, one launch (start us, length us, event | category | flops | bytes accessed | tf_op | source)
XLA Modules:
  0.0 181.9 jit_solution(924421316838362454)
XLA Ops:
  0.7 176.4 %step.1 = (bf16[256,384]{1,0:T(8,128)(2,1)}, f32[256,384]{1,0:T(8,128)}, f32[8,192]{1,0:T(8,128)}, f32[192,384]{1,0:T(8,128)}, f32[192,384]{1,0:T(8,128)}, /*ind...) custom-call(s32[3]{0:T(128)} %refs_0_.1, ...), custom_call_target="tpu_custom_call" | custom-call | tf_op jit(solution)/shard_map/step/pallas_call | solution.py:1078
  177.0 4.7 %finish.1 = (bf16[256,384]{1,0:T(8,128)(2,1)}, f32[256,384]{1,0:T(8,128)}, f32[192,384]{1,0:T(8,128)}, f32[192,384]{1,0:T(8,128)}, f32[192,384]{1,0:T(8,128)}, /...) custom-call(bf16[256,384]{1,0:T(8,128)(2,1)} %get-tuple-element.38.r, ...), custom_call_target="tpu_custom_call" | custom-call | tf_op jit(solution)/shard_map/finish/pallas_call | solution.py:1122

commit v3 on v2

--- a/solution.py
+++ b/solution.py
@@ -59,6 +59,15 @@
     n = c_ref.shape[0]
     rows, cols = iotas(n)
     strength = c_ref[...]
+    m = n // 2
+    side_rows = lax.broadcasted_iota(jnp.int32, (m, n), 0)
+    wide_cols = lax.broadcasted_iota(jnp.int32, (m, n), 1)
+    side_cols = wide_cols % m
+
+    def diagonal(pair):
+        return [jnp.concatenate([jnp.where(wide_cols < m, part, 0).astype(BF),
+                                 jnp.where(wide_cols >= m, part, 0).astype(BF)], 0) for part in pair]
+
     us2 = []
     for h in range(heads):
         raw = r_ref[:, head_cols(h)]
@@ -68,19 +77,28 @@
         u2 = split(u)
         us2.append(u2)
         low = jnp.where(rows > cols, dot3(u2, u2, 1, 1), 0.0)
-        psi_ref[h] = low
-        inv_ref[h] = jnp.where(rows == cols, 1.0, 0.0) - jnp.where(rows // 2 == cols // 2, low, 0.0)
+        blocks = jnp.concatenate([low[0:m, 0:m], low[m:n, m:n]], 1)
+        psi_ref[h, 0:m, :] = blocks
+        psi_ref[h, m:n, 0:m] = low[m:n, 0:m]
+        inv_ref[h, 0:m, :] = (jnp.where(side_rows == side_cols, 1.0, 0.0)
+                              - jnp.where(side_rows // 2 == side_cols // 2, blocks, 0.0))
 
     def double(step, carry):
-        apart = jnp.right_shift(rows, step) != jnp.right_shift(cols, step)
-        pick = apart & (jnp.right_shift(rows, step + 1) == jnp.right_shift(cols, step + 1))
-        halves = [split(inv_ref[h]) for h in range(heads)]
-        mids = [dot3(split(jnp.where(pick, psi_ref[h], 0.0)), halves[h], 1, 0) for h in range(heads)]
+        apart = jnp.right_shift(side_rows, step) != jnp.right_shift(side_cols, step)
+        pick = apart & (jnp.right_shift(side_rows, step + 1) == jnp.right_shift(side_cols, step + 1))
+        now = [split(inv_ref[h, 0:m, :]) for h in range(heads)]
+        mids = [dot3(split(jnp.where(pick, psi_ref[h, 0:m, :], 0.0)), diagonal(now[h]), 1, 0) for h in range(heads)]
         for h in range(heads):
-            inv_ref[h] = inv_ref[h] - dot3(halves[h], split(mids[h]), 1, 0)
+            inv_ref[h, 0:m, :] = inv_ref[h, 0:m, :] - dot3(now[h], diagonal(split(mids[h])), 1, 0)
         return carry
 
-    lax.fori_loop(1, (n - 1).bit_length(), double, 0)
+    lax.fori_loop(1, (m - 1).bit_length(), double, 0)
+    for h in range(heads):
+        first, second = inv_ref[h, 0:m, 0:m], inv_ref[h, 0:m, m:n]
+        corner = -dot3(split(second), split(dot3(split(psi_ref[h, m:n, 0:m]), split(first), 1, 0)), 1, 0)
+        inv_ref[h, 0:m, m:n] = jnp.zeros((m, m), F32)
+        inv_ref[h, m:n, 0:m] = corner
+        inv_ref[h, m:n, m:n] = second
     er, ec = iotas(HDIM)
     for h in range(heads):
         kin = split(inv_ref[h])
@@ -153,15 +171,16 @@
     cs, rs = head_cols(h), slice(start, start + count)
     rows = start + lax.broadcasted_iota(jnp.int32, (count, n), 0)
     cols = lax.broadcasted_iota(jnp.int32, (count, n), 1)
-    own = doc_of(row * n + rows, len_ref)
-    near_ok = (rows >= cols) & (own == doc_of(row * n + cols, len_ref))
+    key_at = lax.broadcasted_iota(jnp.int32, (1, n), 1)
+    own = doc_of(row * n + start + lax.broadcasted_iota(jnp.int32, (count, 1), 0), len_ref)
+    near_ok = (rows >= cols) & (own == doc_of(row * n + key_at, len_ref))
     q = qt_ref[rs, cs]
     s = jnp.where(near_ok, near_ref[h, rs, :] * scale, neg_big)
     s_ref[0:count, :] = s
     top = jnp.max(s, 1, keepdims=True)
     for r in range(1, hops + 1):
         source = row - r
-        docs = jnp.where(source >= 0, doc_of(source * n + cols, len_ref), -1)
+        docs = jnp.where(source >= 0, doc_of(source * n + key_at, len_ref), -1)
         keys = chain_ref[chain_slot(r, r - 1), :, cs]
         s = jnp.where(own == docs, dot(q, keys, 1, 1) * scale, neg_big)
         s_ref[r * count:(r + 1) * count, :] = s
@@ -592,7 +611,6 @@
         return copies.start(ref, ref, device)
 
     get_gate = [copies.start(R.wg.at[mine_c, :], R.wg_s.at[mine_c, cols_of(j)], near[j]) for j in (1, 2)]
-    get_up = [copies.start(R.wu.at[mine_c, :], R.wu_s.at[mine_c, cols_of(j)], near[j]) for j in (1, 2)]
     load_v = loads.start(R.wv, R.w_s.at[:, pl.ds(3 * width, width)])
     load_w = [loads.start(w.at[:, pl.ds(h * HDIM, HDIM)], R.w_s.at[:, pl.ds((3 * h + m) * HDIM, HDIM)])
               for h in range(heads) for m, w in enumerate((R.wq, R.wk, R.wr))]
@@ -601,6 +619,9 @@
     load_f = [loads.start(R.wg, R.wg_s.at[:, pl.ds(0, ff)]), loads.start(R.wu, R.wu_s.at[:, pl.ds(0, ff)]),
               loads.start(R.wd, R.wd_s.at[pl.ds(0, ff), :])]
 
+    for copy in get_gate:
+        copy.wait_recv()
+    relay = [copies.start(R.wg_s.at[mine_c, cols_of(1)], R.wg_s.at[mine_c, cols_of(3)], near[2])]
     get_x.relay()
     get_x.wait()
     for copy in get_gains:
@@ -631,10 +652,7 @@
     path_fwd_stage(heads, Heads(R.proj, 0), Heads(R.proj, 1), Heads(R.proj, 2), R.c, R.qt, R.kt_s, R.near_s, R.prod_s,
                    R.u, R.inv, R.psi, R.x1, R.y1, send_head)
 
-    for copy in get_gate + get_up:
-        copy.wait_recv()
-    relay = [copies.start(R.wg_s.at[mine_c, cols_of(1)], R.wg_s.at[mine_c, cols_of(3)], near[2]),
-             copies.start(R.wu_s.at[mine_c, cols_of(2)], R.wu_s.at[mine_c, cols_of(3)], near[1])]
+    get_up = [copies.start(R.wu.at[mine_c, :], R.wu_s.at[mine_c, cols_of(j)], near[j]) for j in (1, 2)]
     get_down = [copies.start(R.wd.at[mine_f, :], R.wd_s.at[down_rows(j), :], near[j]) for j in (1, 2)]
 
     for copy in get_v:
@@ -671,15 +689,18 @@
     get_a[0].combine()
     mix(0)
     get_a[1].combine()
-    for copy in relay:
-        copy.wait_recv()
-    shared = [pass_on(ref.at[mine_c, three], sibling) for ref in (R.wg_s, R.wu_s)]
+    for copy in get_up:
+        copy.wait_recv()
+    relay.append(copies.start(R.wu_s.at[mine_c, cols_of(2)], R.wu_s.at[mine_c, cols_of(3)], near[1]))
     for copy in get_down:
         copy.wait_recv()
     relay_d = [copies.start(R.wd_s.at[down_rows(1, 0, 2), :], R.wd_s.at[down_rows(3, 0, 2), :], near[2]),
                copies.start(R.wd_s.at[down_rows(2, 1, 2), :], R.wd_s.at[down_rows(3, 1, 2), :], near[1])]
     mix(1)
     get_i[0].relay()
+    for copy in relay:
+        copy.wait_recv()
+    shared = [pass_on(ref.at[mine_c, three], sibling) for ref in (R.wg_s, R.wu_s)]
     for copy in relay_d:
         copy.wait_recv()
     shared += [pass_on(R.wd_s.at[down_rows(j), :], sibling) for j in (1, 2, 3)]
@@ -842,7 +863,7 @@
     left_of(R.gz, R.twin_gz)
 
     fine = piece // 2
-    get_h = []
+    get_h = {}
 
     def rows_at(j, lot):
         return aligned(turned(place.hid, j) * piece + lot * fine, fine, 32)
@@ -850,7 +871,7 @@
     def round_one(src, slot):
         sent = [copies.start(src.at[rows_at(3, lot), :], R.recv_q.at[slot, 2 * lot + 1], near[lot + 1]) for lot in range(2)]
         keep = [copies.start(src.at[rows_at(lot + 1, lot), :], R.recv_q.at[slot, 2 * lot], near[lot + 1]) for lot in range(2)]
-        get_h.extend(keep)
+        get_h[slot] = keep
         return sent
 
     def round_two(src, slot, sent):
@@ -858,7 +879,7 @@
             sent[lot].wait_recv()
             at = src.at[rows_at(2 - lot, lot), :]
             at[...] = (at[...].astype(F32) + R.recv_q[slot, 2 * lot + 1].astype(F32)).astype(BF)
-            get_h.append(copies.start(at, R.recv_q.at[slot, 4 + lot], near[2 - lot]))
+            get_h[slot].append(copies.start(at, R.recv_q.at[slot, 4 + lot], near[2 - lot]))
 
     R.wide_s[...] = dot(R.left_t[:, 0:n], R.o[...], 1, 0) + dot(R.left_t[:, n:2 * n], R.twin_o[...], 1, 0)
     R.d_out[...] = R.wide_s[aligned(place.hid * piece, piece, 64), :]
@@ -971,15 +992,25 @@
         out = out + R.recv_f[slot].astype(F32)
     R.output_s[...] = out.astype(BF)
     stores.append(loads.start(R.output_s, R.output))
+    def final(slot, refs_of):
+        for copy in get_h[slot]:
+            copy.wait_recv()
+        for m, (ref, at) in enumerate(refs_of):
+            for lot in range(2):
+                rs = slice(lot * fine, (lot + 1) * fine)
+                ref[rs, at] = (ref[rs, at] + R.recv_q[slot, 2 * lot, :, head_cols(m)].astype(F32)
+                               + R.recv_q[slot, 4 + lot, :, head_cols(m)].astype(F32))
+
+    final(slot_o, [(R.d_out, head_cols(m)) for m in range(heads)])
     gain = R.gpart[:, window(place.row)]
     for i, copy in enumerate(get_gain):
         copy.wait_recv()
         gain = gain + R.recv_gain[i]
     R.gain_s[...] = gain
     get_gain2 = [copies.start(R.gain_s, R.recv_gain2.at[slot], d) for slot, d in enumerate(to_wid)]
+    round_two(grad_part(heads - 1), heads - 1, sent_h[heads - 1])
     round_two(grad_part(slot_v), slot_v, sent_v)
 
-    round_two(grad_part(heads - 1), heads - 1, sent_h[heads - 1])
     g_act = get_n.total(R.own_n[...])
     stats = R.stat_s[...]
     for slot in range(wid_n - 1):
@@ -989,15 +1020,12 @@
     normed = R.xall[:, my_cols].astype(F32) * inv_rms
     R.d_inputs[...] = (R.gz[:, my_cols].astype(F32)
                        + inv_rms * (g_act * R.gall[0:1, my_cols] - normed * mean))
-    for copy in get_h + get_b:
-        copy.wait_recv()
-    out_outs = [(R.d_out, head_cols(m)) for m in range(heads)]
-    for slot, refs_of in [(slot_o, out_outs), (slot_v, val_outs)] + [(h, outs_of(h)) for h in range(heads)]:
-        for m, (ref, at) in enumerate(refs_of):
-            for lot in range(2):
-                rs = slice(lot * fine, (lot + 1) * fine)
-                ref[rs, at] = (ref[rs, at] + R.recv_q[slot, 2 * lot, :, head_cols(m)].astype(F32)
-                               + R.recv_q[slot, 4 + lot, :, head_cols(m)].astype(F32))
+    for h in range(heads - 1):
+        final(h, outs_of(h))
+    final(heads - 1, outs_of(heads - 1))
+    final(slot_v, val_outs)
+    for copy in get_b:
+        copy.wait_recv()
     d_beta = R.beta_s[:, window(place.hid)]
     for i in range(hid_n - 1):
         d_beta = d_beta + R.recv_b[i]
@@ -1094,7 +1122,7 @@
     loads, stores = [], []
     for a, b, c in zip(ins[:count], bufs[:count], outs[:count]):
         rows = a.shape[0]
-        cut = rows // 2 if rows >= 256 else rows
+        cut = rows // 2 if rows >= 768 else rows
         for start in range(0, rows, cut):
             i, part = len(loads), pl.ds(start, cut)
             loads.append(pltpu.make_async_copy(a.at[part, :], b.at[part, :], sems.at[0, i]))

time: 184 us -> 182 us (0.989)
  no operation moved by 1% of the time
where the time goes in v3:
time: 182 us; the launch traced here: 181 us
  Pallas kernels  181 us (99%)
    pallas_call x1, Pallas kernels, step(): pl.pallas_call(functools.partial(step_kernel, (heads, hops, sizes), ins +...  176 us
    pallas_call x1, Pallas kernels, finish(): pl.pallas_call(functools.partial(finish_kernel, count), in_specs=[spec] *...  4.5 us

profile of v3, /device:TPU:0, one launch (start us, length us, event | category | flops | bytes accessed | tf_op | source)
XLA Modules:
  0.0 181.4 jit_solution(9192377972199389626)
XLA Ops:
  0.7 176.1 %step.1 = (bf16[256,384]{1,0:T(8,128)(2,1)}, f32[256,384]{1,0:T(8,128)}, f32[8,192]{1,0:T(8,128)}, f32[192,384]{1,0:T(8,128)}, f32[192,384]{1,0:T(8,128)}, /*ind...) custom-call(s32[3]{0:T(128)} %refs_0_.1, ...), custom_call_target="tpu_custom_call" | custom-call | tf_op jit(solution)/shard_map/step/pallas_call | solution.py:1106
  176.7 4.5 %finish.1 = (bf16[256,384]{1,0:T(8,128)(2,1)}, f32[256,384]{1,0:T(8,128)}, f32[192,384]{1,0:T(8,128)}, f32[192,384]{1,0:T(8,128)}, f32[192,384]{1,0:T(8,128)}, /...) custom-call(bf16[256,384]{1,0:T(8,128)(2,1)} %get-tuple-element.38.r, ...), custom_call_target="tpu_custom_call" | custom-call | tf_op jit(solution)/shard_map/finish/pallas_call | solution.py:1150

commit v4 on v3

--- a/solution.py
+++ b/solution.py
@@ -939,7 +939,7 @@
             R.grads[0:n, (3 * h + m) * HDIM:(3 * h + m + 1) * HDIM] = val
         gs = pl.ds(h * width, width)
         twin_h.append(copies.start(R.grads.at[pl.ds(0, n), gs], R.grads.at[pl.ds(n, n), gs], sibling))
-        if 0 < h < heads - 1:
+        if 0 < h:
             twin_h[h - 1].wait_recv()
             sent_h.append(weights_of(h - 1, outs_of(h - 1)))
     R.gcs[0:n, :] = gc_all.astype(BF)
@@ -977,7 +977,7 @@
     R.beta_s[...] = d_beta[0:8, :]
     get_b = [copies.start(R.beta_s.at[:, window(turned(place.hid, j))], R.recv_b.at[j - 1], near[j])
              for j in range(1, hid_n)]
-    for h in (heads - 2, heads - 1):
+    for h in (heads - 1,):
         twin_h[h].wait_recv()
         sent_h.append(weights_of(h, outs_of(h)))
     get_n.combine()

time: 182 us -> 181 us (level)
  Pallas kernels: 181 us -> 179 us
where the time goes in v4:
time: 181 us; the launch traced here: 180 us
  Pallas kernels  179 us (99%)
    pallas_call x1, Pallas kernels, step(): pl.pallas_call(functools.partial(step_kernel, (heads, hops, sizes), ins +...  175 us
    pallas_call x1, Pallas kernels, finish(): pl.pallas_call(functools.partial(finish_kernel, count), in_specs=[spec] *...  4.5 us

profile of v4, /device:TPU:0, one launch (start us, length us, event | category | flops | bytes accessed | tf_op | source)
XLA Modules:
  0.0 180.3 jit_solution(10056351687376886560)
XLA Ops:
  0.7 174.9 %step.1 = (bf16[256,384]{1,0:T(8,128)(2,1)}, f32[256,384]{1,0:T(8,128)}, f32[8,192]{1,0:T(8,128)}, f32[192,384]{1,0:T(8,128)}, f32[192,384]{1,0:T(8,128)}, /*ind...) custom-call(s32[3]{0:T(128)} %refs_0_.1, ...), custom_call_target="tpu_custom_call" | custom-call | tf_op jit(solution)/shard_map/step/pallas_call | solution.py:1106
  175.6 4.5 %finish.1 = (bf16[256,384]{1,0:T(8,128)(2,1)}, f32[256,384]{1,0:T(8,128)}, f32[192,384]{1,0:T(8,128)}, f32[192,384]{1,0:T(8,128)}, f32[192,384]{1,0:T(8,128)}, /...) custom-call(bf16[256,384]{1,0:T(8,128)(2,1)} %get-tuple-element.38.r, ...), custom_call_target="tpu_custom_call" | custom-call | tf_op jit(solution)/shard_map/finish/pallas_call | solution.py:1150
